TPU v7x, 32 devices: a whole 2x2x4 slice. The times are simulated.
32 devices in a mesh: row: 2 (over x), col: 16 (over z, y, core).
Axes of the slice: x: 2, y: 2, z: 4, core: 2. Of those that a mesh axis runs over, the one named last changes fastest.
Arguments:
- tokens: bfloat16 [16384, 1024], P('col'), may hold values from -40 to 40
- segment_ids: int32 [16384], P('col'), may hold values from 0 to 127, as said below
- qkv_weight: bfloat16 [1, 1024, 3, 1024], P(None, 'col', None, 'row'), may hold values from -0.1875 to 0.1875
- attn_bias: float32 [1, 2, 1024], P(None, None, 'row'), may hold values from -3 to 3
- out_weight: bfloat16 [1, 1024, 1024], P(None, 'row', 'col'), may hold values from -0.1875 to 0.1875
- ffn_in: bfloat16 [1, 1024, 4096], P(None, 'col', 'row'), may hold values from -0.1875 to 0.1875
- ffn_bias: float32 [1, 4096], P(None, 'row'), may hold values from -3 to 3
- ffn_out: bfloat16 [1, 4096, 1024], P(None, 'row', 'col'), may hold values from -0.09375 to 0.09375
- norm_gain: float32 [1, 2, 1024], replicated, may hold values from 0.5 to 1.5
- shift: float32 [1, 4, 1024], replicated, may hold values from -3 to 3
- cross_weight: bfloat16 [2, 1024, 2, 1024], P(None, 'col', None, 'row'), may hold values from -0.1875 to 0.1875
- page_owner: int32 [1024, 1], P('col'), may hold values from 0 to 15; in each aligned block of 64 rows (0 to 63, 64 to 127, ...) at most 8 rows name the same one
- cache_base: int32 [16], replicated, may hold values from 0 to 15
Outputs:
- encoded: bfloat16 [16384, 1024], P('col', 'row')
- kv_cache: bfloat16 [2, 36864, 2, 1024], P(None, 'col', None, 'row')
Inputs may be any that keep to these rules, and one draw needn't show every extreme that they name: `segment_ids`: each request's tokens are consecutive and lie within one block of 1024 tokens (those of one index of col); block b holds requests b * 8 to b * 8 + 7 in order, each of at most 512 tokens, and some request has exactly 512. `page_owner`: among the 64 pages of one index of col, at most 8 name the same owner.
All inputs are finite; a program needn't handle non-finite values.
Results may differ from a plain program's by a relative error of at most 0.019.
Values may be sent and summed in bfloat16 or wider, within the bound.
A program may use at most 128 MiB of HBM per device.

v0:
```python
import jax
import jax.numpy as jnp
from jax import lax
from jax.sharding import PartitionSpec as P

HDIM = 64
PAGE = 16
BASE_MAX = 16


EPSILON = 1e-05
NEGATIVE = -1e30


def entering(value, axis, join, neutral):
    count, mine = (lax.axis_size(axis), lax.axis_index(axis))
    pieces = lax.all_gather(value, axis)
    so_far = jnp.full_like(value, 0) + jnp.asarray(neutral, value.dtype)

    def hop(position, so_far):
        longer = join(so_far, pieces[position])
        return jnp.where(position < mine, longer, so_far)

    return lax.fori_loop(0, count - 1, hop, so_far)


def add_counts(earlier_part, later_part):
    return earlier_part + later_part


def normalize(summed, scaling_gain, offset_row, moments, feature_width):
    average = moments[0] / feature_width
    variance = moments[1] / feature_width - average * average
    return ((summed - average) * lax.rsqrt(variance + EPSILON) * scaling_gain + offset_row).astype(
        jnp.bfloat16
    )


def settle(partial_value, residual, shift_first, gain_row, shift_second, after_attention):
    feature_width = partial_value.shape[1]
    share_width = feature_width // lax.axis_size("row")
    first_col = lax.axis_index("row") * share_width
    if after_attention:
        combined = lax.psum_scatter(
            partial_value.astype(jnp.bfloat16), "row", scatter_dimension=1, tiled=True
        ).astype(jnp.float32)
    else:
        combined = lax.psum_scatter(
            partial_value.astype(jnp.bfloat16), "row", scatter_dimension=1, tiled=True
        ).astype(jnp.float32)
    own_residual = lax.dynamic_slice_in_dim(residual, first_col, share_width, 1)
    own_shift = lax.dynamic_slice_in_dim(shift_first, first_col, share_width, 0)
    summed = own_residual.astype(jnp.float32) + combined + own_shift
    own_moments = (
        jnp.sum(summed, axis=1, keepdims=True),
        jnp.sum(summed * summed, axis=1, keepdims=True),
    )
    if after_attention:
        moments = lax.psum((own_moments[0], own_moments[1]), "row")
    else:
        moments = lax.psum((own_moments[0], own_moments[1]), "row")
    own_gain = lax.dynamic_slice_in_dim(gain_row, first_col, share_width, 0)
    own_offset = lax.dynamic_slice_in_dim(shift_second, first_col, share_width, 0)
    own_part = normalize(summed, own_gain, own_offset, moments, feature_width)
    if after_attention:
        whole_rows = lax.all_gather(own_part, "row", axis=1, tiled=True)
    else:
        whole_rows = lax.all_gather(own_part, "row", axis=1, tiled=True)
    return (own_part, whole_rows)


def attend(queries, key_rows, values, segment, block_rows):
    token_count = queries.shape[0]
    block_count = token_count // block_rows
    query_blocks = queries.reshape(block_count, block_rows, queries.shape[1], queries.shape[2])
    segment_blocks = segment.reshape(block_count, block_rows)

    def attend_block(inputs):
        query_block, segment_block = inputs
        scores = jnp.einsum(
            "qhd,khd->hqk", query_block, key_rows, preferred_element_type=jnp.float32
        )
        allowed = segment_block[:, None] == segment[None, :]
        scores = jnp.where(allowed[None], scores, NEGATIVE)
        highest = jnp.max(scores, axis=2, keepdims=True)
        exponent = jnp.exp(scores - highest)
        probabilities = (exponent / jnp.sum(exponent, axis=2, keepdims=True)).astype(jnp.bfloat16)
        return jnp.einsum(
            "hqk,khd->qhd", probabilities, values, preferred_element_type=jnp.float32
        ).astype(jnp.bfloat16)

    context = lax.map(attend_block, (query_blocks, segment_blocks))
    return context.reshape(token_count, queries.shape[1] * queries.shape[2])


def per_device(
    tokens,
    segment_ids,
    qkv_weight,
    attn_bias,
    out_weight,
    ffn_in,
    ffn_bias,
    ffn_out,
    norm_gain,
    shift,
    cross_weight,
    page_owner,
    cache_base,
):
    token_count = tokens.shape[0]
    whole_rows = tokens
    source = whole_rows
    local_width = qkv_weight.shape[3]
    columns = source
    projected = jnp.einsum(
        "tn,nkh->tkh",
        columns,
        lax.all_gather(qkv_weight[0], "col", axis=0, tiled=True),
        preferred_element_type=jnp.float32,
    )
    scaling = HDIM ** (-0.5)
    head_count = local_width // HDIM
    queries = (
        ((projected[:, 0] + attn_bias[0, 0]) * scaling)
        .astype(jnp.bfloat16)
        .reshape(token_count, head_count, HDIM)
    )
    key_rows = projected[:, 1].astype(jnp.bfloat16).reshape(token_count, head_count, HDIM)
    values = (
        (projected[:, 2] + attn_bias[0, 1])
        .astype(jnp.bfloat16)
        .reshape(token_count, head_count, HDIM)
    )
    context = attend(queries, key_rows, values, segment_ids, min(512, token_count))
    partial_value = jnp.dot(
        context,
        lax.all_gather(out_weight[0], "col", axis=1, tiled=True),
        preferred_element_type=jnp.float32,
    )
    own_part, normed = settle(
        partial_value, source, shift[0, 0], norm_gain[0, 0], shift[0, 1], True
    )
    columns = normed
    hidden_sum = jnp.dot(
        columns,
        lax.all_gather(ffn_in[0], "col", axis=0, tiled=True),
        preferred_element_type=jnp.float32,
    )
    hidden = jax.nn.gelu(hidden_sum + ffn_bias[0], approximate=False).astype(jnp.bfloat16)
    partial_down = jnp.dot(
        hidden,
        lax.all_gather(ffn_out[0], "col", axis=1, tiled=True),
        preferred_element_type=jnp.float32,
    )
    own_part, whole_rows = settle(
        partial_down, normed, shift[0, 2], norm_gain[0, 1], shift[0, 3], False
    )
    layer_count = cross_weight.shape[0]
    columns = whole_rows
    cross_pairs = jnp.einsum(
        "tn,dnkh->dtkh",
        columns,
        lax.all_gather(cross_weight, "col", axis=1, tiled=True),
        preferred_element_type=jnp.float32,
    ).astype(jnp.bfloat16)
    owners = page_owner[:, 0]
    page_count = owners.shape[0]
    owner_count = lax.axis_size("col")
    capacity = max(2, (2 * page_count + owner_count - 1) // owner_count)
    owner_ids = jnp.arange(owner_count, dtype=jnp.int32)
    onehot = (owners[:, None] == owner_ids[None, :]).astype(jnp.int32)
    counts = jnp.sum(onehot, axis=0)
    earlier = entering(counts, "col", add_counts, jnp.zeros_like(counts))
    local_rank = jnp.sum((jnp.cumsum(onehot, axis=0) - onehot) * onehot, axis=1)
    slot_index = jnp.sum(onehot * (cache_base + earlier)[None, :], axis=1) + local_rank
    target = owners * capacity + local_rank
    send_ids = jnp.arange(owner_count * capacity, dtype=jnp.int32)
    chosen = (send_ids[:, None] == target[None, :]).astype(jnp.int32)
    outgoing_slot = jnp.where(
        jnp.sum(chosen, axis=1) > 0, jnp.sum(chosen * slot_index[None, :], axis=1), -1
    )
    page_rows = cross_pairs.reshape(layer_count, page_count, -1)
    outgoing = jnp.einsum(
        "sp,dpx->sdx", chosen.astype(jnp.bfloat16), page_rows, preferred_element_type=jnp.float32
    ).astype(jnp.bfloat16)
    arrived, arrived_slot = (
        lax.all_to_all(outgoing, "col", split_axis=0, concat_axis=0, tiled=True),
        lax.all_to_all(outgoing_slot, "col", split_axis=0, concat_axis=0, tiled=True),
    )
    own_pages = BASE_MAX + capacity * owner_count
    placer = (jnp.arange(own_pages, dtype=jnp.int32)[:, None] == arrived_slot[None, :]).astype(
        jnp.bfloat16
    )
    cache_rows = jnp.einsum(
        "ws,sdx->dwx", placer, arrived, preferred_element_type=jnp.float32
    ).astype(jnp.bfloat16)
    return (own_part, cache_rows.reshape(layer_count, own_pages * PAGE, 2, cross_weight.shape[3]))


def solution(mesh):
    return jax.shard_map(
        per_device,
        mesh=mesh,
        in_specs=(
            P("col", None),
            P("col"),
            P(None, "col", None, "row"),
            P(None, None, "row"),
            P(None, "row", "col"),
            P(None, "col", "row"),
            P(None, "row"),
            P(None, "row", "col"),
            P(),
            P(),
            P(None, "col", None, "row"),
            P("col", None),
            P(),
        ),
        out_specs=(P("col", "row"), P(None, "col", None, "row")),
        check_vma=False,
    )
```

profile of v0, /device:TPU:13, one launch (start us, length us, event | category | flops | bytes accessed | tf_op | source)
XLA Modules:
  0.0 739.3 jit_solution(158126474984680303)
XLA Ops:
  10.3 46.1 %all-gather.19.cloned.1.call-done = bf16[1,1024,3,512]{3,1,2,0:T(8,128)(2,1)} async-done(((bf16[1,64,3,512]{3,1,2,0:T(8,128)(2,1)}), bf16[1,1024,3,512]{3,1,2,0:T(8,128)(2,1)}) %all-gather.19.cloned.1.call-update) | async-done | bytes 3145744 | tf_op jit(solution)/shard_map/all_gather | solution.py:119
  56.5 6.2 fusion.66
  64.5 3.0 squeeze.42
  72.4 76.3 %while.24 = (s32[]{:T(128)}, bf16[2,512,8,64]{1,3,2,0:T(8,128)(2,1)}, s32[2,512]{1,0:T(2,128)S(1)}, s32[1024]{0:T(1024)S(1)}, bf16[2,512,8,64]{1,3,2,0:T(8,128)(...) while((s32[]{:T(128)}, bf16[2,512,8,64]{1,3,2,0:T(8,128)(2,1)}, ...), condition=%wide.region_3.4_spmd, body=%wide.region_0.3_spmd.sunk | while | flops 1099695104 | bytes 71346776 | solution.py:92
  72.4 8.1 %fusion.140 = f32[8,512,1024]{2,1,0:T(8,128)} fusion(bf16[1024,8,64]{0,2,1:T(8,128)(2,1)S(1)} %get-tuple-element.284, bf16[2,512,8,64]{1,3,2,0:T(8,128)(2,1)S(1)} %get-tuple-element.283, s32[]{:T(128)} %get-tuple-element.271), kind=kOutput, calls=%fused_computation.12.clone.1 | convolution fusion | flops 536870912 | bytes 18350084 | tf_op jit(solution)/shard_map/while/body/eval_jaxpr/qhd,khd->hqk/dot_general | solution.py:80
  80.9 20.0 %fusion.141 = (f32[8,512]{1,0:T(8,128)S(1)}, f32[8,512,1024]{2,1,0:T(8,128)}) fusion(f32[8,512,1024]{2,1,0:T(8,128)} %fusion.140, pred[512,1024]{1,0:T(8,128)(4,1)S(1)} %broadcast_compare_fusion.2), kind=kOutput, calls=%fused_computation.156.clone.1 | output fusion | flops 16778240 | bytes 34095104 | tf_op jit(solution)/shard_map/while/body/eval_jaxpr/sub | solution.py:86
  100.8 9.5 %fusion.142 = bf16[2,512,8,64]{1,3,2,0:T(8,128)(2,1)} fusion(bf16[2,512,8,64]{1,3,2,0:T(8,128)(2,1)} %get-tuple-element.272, s32[]{:T(128)} %get-tuple-element.271, bf16[1024,8,64]{0,2,1:T(8,128)(2,1)} %get-tuple-element.285, f32[8,512,1024]{2,1,0:T(8,128)} %get-tuple-element.257, f32[8,512]{1,0:T(8,128)S(1)} %get-tuple-element.258), kind=kOutput, calls=%fused_computation.10.clone.1 | convolution fusion | flops 545521664 | bytes 18366976 | tf_op jit(solution)/shard_map/while/body/eval_jaxpr/hqk,khd->qhd/dot_general | solution.py:88
  110.3 8.1 %fusion.140 = f32[8,512,1024]{2,1,0:T(8,128)} fusion(bf16[1024,8,64]{0,2,1:T(8,128)(2,1)S(1)} %get-tuple-element.284, bf16[2,512,8,64]{1,3,2,0:T(8,128)(2,1)S(1)} %get-tuple-element.283, s32[]{:T(128)} %get-tuple-element.271), kind=kOutput, calls=%fused_computation.12.clone.1 | convolution fusion | flops 536870912 | bytes 18350084 | tf_op jit(solution)/shard_map/while/body/eval_jaxpr/qhd,khd->hqk/dot_general | solution.py:80
  118.8 20.0 %fusion.141 = (f32[8,512]{1,0:T(8,128)S(1)}, f32[8,512,1024]{2,1,0:T(8,128)}) fusion(f32[8,512,1024]{2,1,0:T(8,128)} %fusion.140, pred[512,1024]{1,0:T(8,128)(4,1)S(1)} %broadcast_compare_fusion.2), kind=kOutput, calls=%fused_computation.156.clone.1 | output fusion | flops 16778240 | bytes 34095104 | tf_op jit(solution)/shard_map/while/body/eval_jaxpr/sub | solution.py:86
  138.8 9.5 %fusion.142 = bf16[2,512,8,64]{1,3,2,0:T(8,128)(2,1)} fusion(bf16[2,512,8,64]{1,3,2,0:T(8,128)(2,1)} %get-tuple-element.272, s32[]{:T(128)} %get-tuple-element.271, bf16[1024,8,64]{0,2,1:T(8,128)(2,1)} %get-tuple-element.285, f32[8,512,1024]{2,1,0:T(8,128)} %get-tuple-element.257, f32[8,512]{1,0:T(8,128)S(1)} %get-tuple-element.258), kind=kOutput, calls=%fused_computation.10.clone.1 | convolution fusion | flops 545521664 | bytes 18366976 | tf_op jit(solution)/shard_map/while/body/eval_jaxpr/hqk,khd->qhd/dot_general | solution.py:88
  151.5 3.9 convolution_convert_fusion.2
  156.7 29.6 %reduce-scatter.3.cloned.1.call-done = bf16[1024,512]{1,0:T(8,128)(2,1)} async-done(((bf16[1024,1024]{1,0:T(8,128)(2,1)}), bf16[1024,512]{1,0:T(8,128)(2,1)}) %reduce-scatter.3.cloned.1.call-update) | async-done | bytes 1048592 | tf_op jit(solution)/shard_map/reduce_scatter | solution.py:44
  188.0 3.9 all-reduce.2
  194.8 43.8 %all-gather.23.cloned.1.call-done = bf16[1,1024,2048]{2,1,0:T(8,128)(2,1)} async-done(((bf16[1,64,2048]{2,1,0:T(8,128)(2,1)}), bf16[1,1024,2048]{2,1,0:T(8,128)(2,1)}) %all-gather.23.cloned.1.call-update) | async-done | bytes 4194320 | tf_op jit(solution)/shard_map/all_gather | solution.py:147
  238.6 51.3 %all-gather.25.cloned.1.call-done = bf16[1,2048,1024]{1,2,0:T(8,128)(2,1)} async-done(((bf16[1,2048,64]{1,2,0:T(8,128)(2,1)}), bf16[1,2048,1024]{1,2,0:T(8,128)(2,1)}) %all-gather.25.cloned.1.call-update) | async-done | bytes 4194320 | tf_op jit(solution)/shard_map/all_gather | solution.py:153
  289.9 34.2 %all-gather.13.cloned.1.call-done = bf16[1024,1024]{1,0:T(8,128)(2,1)} async-done(((bf16[1024,512]{1,0:T(8,128)(2,1)}), bf16[1024,1024]{1,0:T(8,128)(2,1)}) %all-gather.13.cloned.1.call-update) | async-done | bytes 2097168 | tf_op jit(solution)/shard_map/all_gather | solution.py:66
  324.1 29.5 %fusion.72 = bf16[1024,1024]{1,0:T(8,128)(2,1)} fusion(bf16[1,2048,1024]{1,2,0:T(8,128)(2,1)} %all-gather.25.cloned.1.call-done, bf16[1024,1024]{1,0:T(8,128)(2,1)} %all-gather.13.cloned.1.call-done, bf16[1,1024,2048]{2,1,0:T(8,128)(2,1)} %all-gather.23.cloned.1.call-done, f32[2048]{0:T(1024)S(1)} %bitcast.122), kind=kOutput, calls=%fused_computation.94 | convolution fusion | flops 8729395200 | bytes 12591104 | tf_op jit(solution)/shard_map/dot_general | solution.py:151
  356.2 7.9 %all-reduce = s32[256]{0:T(256)S(1)} all-reduce(s32[256]{0:T(256)S(1)} %dynamic-update-slice), channel_id=6, replica_groups=mesh['row'=2,'col'=16] {'col'}, use_global_device_ids=true, to_apply=%add | all-reduce | flops 256 | bytes 2048
  364.1 21.5 %reduce-scatter.5.cloned.1.call-done = bf16[1024,512]{1,0:T(8,128)(2,1)} async-done(((bf16[1024,1024]{1,0:T(8,128)(2,1)}), bf16[1024,512]{1,0:T(8,128)(2,1)}) %reduce-scatter.5.cloned.1.call-update) | async-done | bytes 1048592 | tf_op jit(solution)/shard_map/reduce_scatter | solution.py:48
  387.4 3.9 all-reduce.1
  395.9 7.5 %all-to-all-start.1 = ((s32[16,8,1]{1,2,0:T(1,128)}), s32[16,8,1]{1,2,0:T(1,128)S(1)}, u32[]{:S(2)}, u32[]{:S(2)}) async-start(s32[16,8,1]{1,2,0:T(1,128)} %bitcast.32), calls=%async_computation.3 | async-start | bytes 16384 | tf_op jit(solution)/shard_map/all_to_all | solution.py:189
  403.5 34.8 %all-gather.17.cloned.1.call-done = bf16[2,1024,2,512]{3,1,2,0:T(8,128)(2,1)} async-done(((bf16[2,64,2,512]{3,1,2,0:T(8,128)(2,1)}), bf16[2,1024,2,512]{3,1,2,0:T(8,128)(2,1)}) %all-gather.17.cloned.1.call-update) | async-done | bytes 4194320 | tf_op jit(solution)/shard_map/all_gather | solution.py:164
  438.2 34.3 %all-gather.15.cloned.1.call-done = bf16[1024,1024]{1,0:T(8,128)(2,1)} async-done(((bf16[1024,512]{1,0:T(8,128)(2,1)}), bf16[1024,1024]{1,0:T(8,128)(2,1)}) %all-gather.15.cloned.1.call-update) | async-done | bytes 2097168 | tf_op jit(solution)/shard_map/all_gather | solution.py:68
  472.5 7.3 convert_bitcast_fusion
  479.8 6.3 copy.27
  486.1 7.8 %reshape.128 = bf16[2,64,16384]{2,1,0:T(8,128)(2,1)} reshape(bf16[2,1024,2,512]{3,2,1,0:T(2,128)(2,1)} %copy.27) | data formatting | bytes 8388608 | tf_op jit(solution)/shard_map/reshape | solution.py:183
  493.9 4.6 convolution_convert_fusion.1
  498.5 15.4 %copy.28 = bf16[128,2,16384]{2,1,0:T(2,128)(2,1)} copy(bf16[128,2,16384]{2,0,1:T(8,128)(2,1)S(1)} %convolution_convert_fusion.1) | data formatting | bytes 16777216 | tf_op jit(solution)/shard_map/convert_element_type | solution.py:186
  514.0 6.8 all-to-all-start
  522.1 180.8 %all-to-all-done = bf16[128,2,16384]{2,1,0:T(2,128)(2,1)} async-done(((bf16[128,2,16384]{2,1,0:T(2,128)(2,1)}), bf16[128,2,16384]{2,1,0:T(2,128)(2,1)}, u32[]{:S(2)}, u32[]{:S(2)}) %all-to-all-start) | async-done | bytes 8388640 | tf_op jit(solution)/shard_map/all_to_all | solution.py:188
  702.9 13.5 %fusion.15 = bf16[2,144,16384]{2,1,0:T(8,128)(2,1)} fusion(bf16[128,2,16384]{2,1,0:T(2,128)(2,1)} %all-to-all-done, s32[128]{0:T(128)S(1)} %eq.67), kind=kOutput, calls=%fused_computation.22 | convolution fusion | flops 1212696576 | bytes 17826304 | tf_op jit(solution)/shard_map/ws,sdx->dwx/dot_general | solution.py:195
  716.4 16.1 %reshape.129 = bf16[2,2304,2,512]{3,2,1,0:T(2,128)(2,1)} reshape(bf16[2,144,16384]{2,1,0:T(8,128)(2,1)} %fusion.15) | data formatting | bytes 18874368 | tf_op jit(solution)/shard_map/reshape | solution.py:198
  (101 shorter events, 29.1 us)
Async XLA Ops:
  7.2 49.3 %all-gather.19.cloned.1.call-start = ((), (), s32[]{:S(2)}) async-start(), calls=%async_computation.9 | async-start | bytes 3342336 | tf_op jit(solution)/shard_map/all_gather | solution.py:119
  7.9 143.6 %all-gather.21.cloned.1.call-start = ((), (), s32[]{:S(2)}) async-start(), calls=%async_computation.10 | async-start | bytes 1114112 | tf_op jit(solution)/shard_map/all_gather | solution.py:138
  8.6 177.6 %reduce-scatter.3.cloned.1.call-start = ((), (), s32[]{:S(2)}) async-start(), calls=%async_computation.4 | async-start | bytes 3145728 | tf_op jit(solution)/shard_map/reduce_scatter | solution.py:44
  64.4 8.0 %copy-start.3 = (s32[1024]{0:T(1024)S(1)}, s32[1024]{0:T(1024)}, u32[]{:S(2)}) copy-start(s32[1024]{0:T(1024)} %param.18) | copy-start | bytes 12292
  148.7 7.9 %copy-start.5 = (f32[1,2,1024]{2,1,0:T(2,128)S(1)}, f32[1,2,1024]{2,1,0:T(2,128)}, u32[]{:S(2)}) copy-start(f32[1,2,1024]{2,1,0:T(2,128)} %param.25) | copy-start | bytes 24580
  148.7 7.9 %copy-start.4 = (f32[1,4,1024]{2,1,0:T(4,128)S(1)}, f32[1,4,1024]{2,1,0:T(4,128)}, u32[]{:S(2)}) copy-start(f32[1,4,1024]{2,1,0:T(4,128)} %param.26) | copy-start | bytes 49156
  148.7 37.5 %copy-start = (bf16[1024,1024]{1,0:T(8,128)(2,1)S(1)}, bf16[1024,1024]{1,0:T(8,128)(2,1)}, u32[]{:S(2)}) copy-start(bf16[1024,1024]{1,0:T(8,128)(2,1)} %param.17) | copy-start | bytes 6291460
  151.5 172.6 %copy-start.7 = (f32[1,2048]{1,0:T(1,128)S(1)}, f32[1,2048]{1,0:T(1,128)}, u32[]{:S(2)}) copy-start(f32[1,2048]{1,0:T(1,128)} %param.23) | copy-start | bytes 24580
  155.3 83.2 %all-gather.23.cloned.1.call-start = ((), (), s32[]{:S(2)}) async-start(), calls=%async_computation.11 | async-start | bytes 4456448 | tf_op jit(solution)/shard_map/all_gather | solution.py:147
  155.9 134.0 %all-gather.25.cloned.1.call-start = ((), (), s32[]{:S(2)}) async-start(), calls=%async_computation.12 | async-start | bytes 4456448 | tf_op jit(solution)/shard_map/all_gather | solution.py:153
  156.5 167.6 %all-gather.13.cloned.1.call-start = ((), (), s32[]{:S(2)}) async-start(), calls=%async_computation.5 | async-start | bytes 3145728 | tf_op jit(solution)/shard_map/all_gather | solution.py:66
  194.7 190.9 %reduce-scatter.5.cloned.1.call-start = ((), (), s32[]{:S(2)}) async-start(), calls=%async_computation.6 | async-start | bytes 3145728 | tf_op jit(solution)/shard_map/reduce_scatter | solution.py:48
  324.1 29.6 %copy-start.2 = (bf16[2,64,2,512]{3,2,1,0:T(2,128)(2,1)S(1)}, bf16[2,64,2,512]{3,2,1,0:T(2,128)(2,1)}, u32[]{:S(2)}) copy-start(bf16[2,64,2,512]{3,2,1,0:T(2,128)(2,1)} %param.27) | copy-start | bytes 786436
  324.1 30.5 %copy-start.9 = (u32[32]{0:T(128)S(1)}, u32[32]{0:T(128)}, u32[]{:S(2)}) copy-start(u32[32]{0:T(128)} %constant.147) | copy-start | bytes 388
  324.1 31.7 %copy-start.6 = (s32[64,1]{0,1:T(1,128)S(1)}, s32[64,1]{0,1:T(1,128)}, u32[]{:S(2)}) copy-start(s32[64,1]{0,1:T(1,128)} %param.28) | copy-start | bytes 772
  324.1 61.5 %copy-start.1 = (bf16[1024,1024]{1,0:T(8,128)(2,1)S(1)}, bf16[1024,1024]{1,0:T(8,128)(2,1)}, u32[]{:S(2)}) copy-start(bf16[1024,1024]{1,0:T(8,128)(2,1)} %all-gather.13.cloned.1.call-done) | copy-start | bytes 6291460
  353.6 41.3 %copy-start.8 = (s32[16]{0:T(128)S(1)}, s32[16]{0:T(128)}, u32[]{:S(2)}) copy-start(s32[16]{0:T(128)} %param.29) | copy-start | bytes 196
  353.7 84.6 %all-gather.17.cloned.1.call-start = ((), (), s32[]{:S(2)}) async-start(), calls=%async_computation.8 | async-start | bytes 4456448 | tf_op jit(solution)/shard_map/all_gather | solution.py:164
  354.5 118.0 %all-gather.15.cloned.1.call-start = ((), (), s32[]{:S(2)}) async-start(), calls=%async_computation.7 | async-start | bytes 3145728 | tf_op jit(solution)/shard_map/all_gather | solution.py:68
  395.9 118.0 %all-to-all-start.1 = ((s32[16,8,1]{1,2,0:T(1,128)}), s32[16,8,1]{1,2,0:T(1,128)S(1)}, u32[]{:S(2)}, u32[]{:S(2)}) async-start(s32[16,8,1]{1,2,0:T(1,128)} %bitcast.32), calls=%async_computation.3 | async-start | bytes 16384 | tf_op jit(solution)/shard_map/all_to_all | solution.py:189
  514.0 189.0 %all-to-all-start = ((bf16[128,2,16384]{2,1,0:T(2,128)(2,1)}), bf16[128,2,16384]{2,1,0:T(2,128)(2,1)}, u32[]{:S(2)}, u32[]{:S(2)}) async-start(bf16[128,2,16384]{2,1,0:T(2,128)(2,1)} %copy.28), calls=%async_computation.2 | async-start | bytes 16777216 | tf_op jit(solution)/shard_map/all_to_all | solution.py:188
Sparse Core Ops, SparseCore 0:
  10.2 46.2 all-gather.18
  58.6 36.0 all-gather.20
  155.5 30.7 reduce-scatter.2
  188.5 50.0 all-gather.22
  240.8 49.0 all-gather.24
  292.0 32.0 all-gather.12
  353.8 31.8 reduce-scatter.4
  387.8 50.3 all-gather.16
  440.3 32.0 all-gather.14
where the time goes:
time: 744 us; the launch traced here: 739 us
  waiting for transfers between devices  479 us (64%)
  matrix products  100 us (13%)
  local copies, waits for them, and re-layouts  58 us (8%)
  other arithmetic  56.2 us (8%)
  blocking collectives  15.6 us (2%)
  between operations  15.1 us (2%)
  starting transfers between devices  14.7 us (2%)
    all_to_all x1, waiting for transfers between devices, per_device(): lax.all_to_all(outgoing, 'col', split_axis=0, concat_axis=0, tiled=True)  181 us
    all_gather x2, waiting for transfers between devices, settle(): whole_rows = lax.all_gather(own_part, 'row', axis=1, tiled=True)  68.4 us
    all_gather x1, waiting for transfers between devices, per_device(): lax.all_gather(ffn_out[0], 'col', axis=1, tiled=True)  51.3 us
    reduce_scatter x2, waiting for transfers between devices, settle(): lax.psum_scatter(partial_value.astype(jnp.bfloat16), 'row', scatter_dimen...  51.1 us
    all_gather x1, waiting for transfers between devices, per_device(): lax.all_gather(qkv_weight[0], 'col', axis=0, tiled=True)  46.1 us
    all_gather x1, waiting for transfers between devices, per_device(): lax.all_gather(ffn_in[0], 'col', axis=0, tiled=True)  43.8 us
    sub x2, other arithmetic, attend_block(): exponent = jnp.exp(scores - highest)  39.9 us
    all_gather x1, waiting for transfers between devices, per_device(): lax.all_gather(cross_weight, 'col', axis=1, tiled=True)  34.8 us
  transfers between devices with their start and end apart: 11, of which 9 were waited for; matrix products, arithmetic and copies ran while one was open for 20% of the time, Pallas kernels for 0%

commit v1 on v0

v1 whole, which is shorter than its diff:
```python
import functools

import jax
import jax.numpy as jnp
from jax import lax
from jax.experimental import pallas as pl
from jax.experimental.pallas import tpu as pltpu
from jax.sharding import PartitionSpec as P

HDIM = 64
PAGE = 16
BASE_MAX = 16
EPSILON = 1e-05
NEGATIVE = -1e30
CHUNKS = 2
MIB = 1 << 20
MESH = pl.DeviceIdType.MESH


def attend_kernel(
    x_ref, w_ref, bias_ref, seg_col_ref, seg_row_ref, out_ref, q_ref, k_ref, v_ref, *, q_rows
):
    x = x_ref[...]
    q = jnp.dot(x, w_ref[0], preferred_element_type=jnp.float32)
    q_ref[...] = ((q + bias_ref[0:1]) * HDIM ** (-0.5)).astype(jnp.bfloat16)
    k = jnp.dot(x, w_ref[1], preferred_element_type=jnp.float32)
    k_ref[...] = k.astype(jnp.bfloat16)
    v = jnp.dot(x, w_ref[2], preferred_element_type=jnp.float32)
    v_ref[...] = (v + bias_ref[1:2]).astype(jnp.bfloat16)
    tokens, width = q_ref.shape

    def block(i, _):
        rows = pl.ds(pl.multiple_of(i * q_rows, q_rows), q_rows)
        allowed = seg_col_ref[rows, :] == seg_row_ref[...]
        parts = []
        for h in range(width // HDIM):
            cols = slice(h * HDIM, (h + 1) * HDIM)
            scores = lax.dot_general(
                q_ref[rows, cols],
                k_ref[:, cols],
                (((1,), (1,)), ((), ())),
                preferred_element_type=jnp.float32,
            )
            scores = jnp.where(allowed, scores, NEGATIVE)
            highest = jnp.max(scores, axis=1, keepdims=True)
            exponent = jnp.exp(scores - highest)
            total = jnp.sum(exponent, axis=1, keepdims=True)
            mixed = jnp.dot(
                exponent.astype(jnp.bfloat16), v_ref[:, cols], preferred_element_type=jnp.float32
            )
            parts.append(mixed / total)
        out_ref[rows, :] = jnp.concatenate(parts, axis=1).astype(jnp.bfloat16)
        return 0

    lax.fori_loop(0, tokens // q_rows, block, 0)


def attention(tokens, weight, bias, segment):
    count, depth = tokens.shape
    width = weight.shape[2]
    step = 256
    return pl.pallas_call(
        functools.partial(attend_kernel, q_rows=256),
        grid=(width // step,),
        in_specs=[
            pl.BlockSpec((count, depth), lambda i: (0, 0)),
            pl.BlockSpec((3, depth, step), lambda i: (0, 0, i)),
            pl.BlockSpec((2, step), lambda i: (0, i)),
            pl.BlockSpec((count, 1), lambda i: (0, 0)),
            pl.BlockSpec((1, count), lambda i: (0, 0)),
        ],
        out_specs=pl.BlockSpec((count, step), lambda i: (0, i)),
        out_shape=jax.ShapeDtypeStruct((count, width), jnp.bfloat16),
        scratch_shapes=[pltpu.VMEM((count, step), jnp.bfloat16)] * 3,
        compiler_params=pltpu.CompilerParams(vmem_limit_bytes=40 * MIB),
        cost_estimate=pl.CostEstimate(
            flops=40 * 10**9, bytes_accessed=6 * MIB, transcendentals=8 * MIB
        ),
        name="attention",
    )(tokens, weight, bias, segment[:, None], segment[None, :])


def dispatch_kernel(n, out_ref, got_ref, local_sem, send_sem, recv_sem, send2_sem, recv2_sem):
    me, side = lax.axis_index("col"), lax.axis_index("row")
    other = 1 - side
    barrier = pltpu.get_barrier_semaphore()
    for k in range(1, n):
        pl.semaphore_signal(
            barrier, inc=1, device_id=(side, lax.rem(me + k, n)), device_id_type=MESH
        )
    pl.semaphore_signal(barrier, inc=1, device_id=(other, me), device_id_type=MESH)
    pl.semaphore_wait(barrier, n)

    def first(k):
        target = lax.rem(me + k, n)
        return pltpu.make_async_remote_copy(
            src_ref=out_ref.at[target],
            dst_ref=got_ref.at[side, me],
            send_sem=send_sem.at[k],
            recv_sem=recv_sem.at[k],
            device_id=(side, target),
            device_id_type=MESH,
        )

    def second(k, source):
        return pltpu.make_async_remote_copy(
            src_ref=source,
            dst_ref=got_ref.at[side, lax.rem(me + n - k, n)],
            send_sem=send2_sem.at[k],
            recv_sem=recv2_sem.at[k],
            device_id=(other, me),
            device_id_type=MESH,
        )

    firsts = [first(k) for k in range(1, n)]
    for copy in firsts:
        copy.start()
    own = pltpu.make_async_copy(out_ref.at[me], got_ref.at[side, me], local_sem)
    own.start()
    seconds = [second(0, out_ref.at[me])]
    seconds[0].start()
    for k in range(1, n):
        firsts[k - 1].wait_recv()
        copy = second(k, got_ref.at[side, lax.rem(me + n - k, n)])
        copy.start()
        seconds.append(copy)
    own.wait()
    for copy in firsts:
        copy.wait_send()
    for copy in seconds:
        copy.wait()


def dispatch(outgoing):
    n, rows, width = outgoing.shape
    return pl.pallas_call(
        functools.partial(dispatch_kernel, n),
        in_specs=[pl.BlockSpec(memory_space=pl.ANY)],
        out_specs=pl.BlockSpec(memory_space=pl.ANY),
        out_shape=jax.ShapeDtypeStruct((2, n, rows, width), outgoing.dtype),
        scratch_shapes=[pltpu.SemaphoreType.DMA(())] + [pltpu.SemaphoreType.DMA((n,))] * 4,
        compiler_params=pltpu.CompilerParams(collective_id=1, has_side_effects=True),
        name="dispatch",
    )(outgoing)


def cache_kernel(index_ref, got_ref, w_ref, out_ref, x_ref, *, pages):
    base = pl.program_id(0) * pages
    half = got_ref.shape[2]
    for j in range(pages):
        at = index_ref[base + j]
        rows = pl.ds(pl.multiple_of(jnp.maximum(at, 0) * PAGE, PAGE), PAGE)
        for s in range(2):
            page = got_ref[s, rows, :]
            page = jnp.where(at >= 0, page, jnp.zeros_like(page))
            x_ref[j * PAGE : (j + 1) * PAGE, s * half : (s + 1) * half] = page
    x = x_ref[...]
    for d in range(w_ref.shape[0]):
        for k in range(2):
            out_ref[d, k] = jnp.dot(x, w_ref[d, k], preferred_element_type=jnp.float32).astype(
                jnp.bfloat16
            )


def fill_cache(index, got, weight, pages):
    own_pages = index.shape[0]
    layers, _, depth, width = weight.shape
    return pl.pallas_call(
        functools.partial(cache_kernel, pages=pages),
        grid_spec=pltpu.PrefetchScalarGridSpec(
            num_scalar_prefetch=1,
            grid=(own_pages // pages,),
            in_specs=[
                pl.BlockSpec(got.shape, lambda i, s: (0, 0, 0)),
                pl.BlockSpec(weight.shape, lambda i, s: (0, 0, 0, 0)),
            ],
            out_specs=pl.BlockSpec((layers, 2, pages * PAGE, width), lambda i, s: (0, 0, i, 0)),
            scratch_shapes=[pltpu.VMEM((pages * PAGE, depth), jnp.bfloat16)],
        ),
        out_shape=jax.ShapeDtypeStruct((layers, 2, own_pages * PAGE, width), jnp.bfloat16),
        compiler_params=pltpu.CompilerParams(vmem_limit_bytes=40 * MIB),
        cost_estimate=pl.CostEstimate(
            flops=10**10, bytes_accessed=18 * MIB, transcendentals=0
        ),
        name="fill_cache",
    )(index, got, weight)


def settle(partial_value, residual, shift_first, gain_row, shift_second):
    mine = partial_value.astype(jnp.bfloat16)
    theirs = lax.ppermute(mine, "row", [(0, 1), (1, 0)])
    summed = (
        residual.astype(jnp.float32)
        + (mine.astype(jnp.float32) + theirs.astype(jnp.float32))
        + shift_first
    )
    average = jnp.mean(summed, axis=1, keepdims=True)
    variance = jnp.mean(summed * summed, axis=1, keepdims=True) - average * average
    return (
        (summed - average) * lax.rsqrt(variance + EPSILON) * gain_row + shift_second
    ).astype(jnp.bfloat16)


def times_transposed(left, right):
    return lax.dot_general(
        left, right, (((1,), (1,)), ((), ())), preferred_element_type=jnp.float32
    )


def per_device(
    tokens,
    segment_ids,
    qkv_weight,
    attn_bias,
    out_weight,
    ffn_in,
    ffn_bias,
    ffn_out,
    norm_gain,
    shift,
    cross_weight,
    page_owner,
    cache_base,
):
    token_count = tokens.shape[0]
    n, me = lax.axis_size("col"), lax.axis_index("col")

    def gather(value, axis):
        return lax.all_gather(value, "col", axis=axis, tiled=True)

    w_qkv = gather(qkv_weight[0].transpose(1, 0, 2), 1)
    w_out = gather(out_weight[0].T, 0)
    w_in = gather(ffn_in[0], 0)
    w_down = gather(ffn_out[0].T, 0)
    w_cross = gather(cross_weight.transpose(0, 2, 1, 3), 2)
    all_owners = lax.all_gather(page_owner[:, 0], "col")

    page_count = page_owner.shape[0]
    capacity = max(2, (2 * page_count + n - 1) // n)
    owner_ids = jnp.arange(n, dtype=jnp.int32)
    owners = page_owner[:, 0]
    onehot = (owners[:, None] == owner_ids[None, :]).astype(jnp.int32)
    local_rank = jnp.sum((jnp.cumsum(onehot, axis=0) - onehot) * onehot, axis=1)
    target = owners * capacity + local_rank
    token_target = (
        target[:, None] * PAGE + jnp.arange(PAGE, dtype=jnp.int32)[None, :]
    ).reshape(token_count)
    chosen = (
        jnp.arange(n * capacity * PAGE, dtype=jnp.int32)[:, None] == token_target[None, :]
    ).astype(jnp.bfloat16)
    received = jnp.sum((all_owners == me).astype(jnp.int32), axis=1)
    earlier = jnp.cumsum(received) - received
    own_base = jnp.sum(jnp.where(owner_ids == me, cache_base, 0))
    place_ids = jnp.arange(capacity, dtype=jnp.int32)
    slots = jnp.where(
        place_ids[None, :] < received[:, None],
        own_base + earlier[:, None] + place_ids[None, :],
        -1,
    ).reshape(n * capacity)
    own_pages = BASE_MAX + capacity * n
    hits = jnp.arange(own_pages, dtype=jnp.int32)[:, None] == slots[None, :]
    page_at = jnp.max(
        jnp.where(hits, jnp.arange(n * capacity, dtype=jnp.int32)[None, :], -1), axis=1
    )

    context = attention(tokens, w_qkv, attn_bias[0], segment_ids)
    rows = token_count // CHUNKS
    encoded = []
    for c in range(CHUNKS):
        part = slice(c * rows, (c + 1) * rows)
        normed = settle(
            times_transposed(context[part], w_out),
            tokens[part],
            shift[0, 0],
            norm_gain[0, 0],
            shift[0, 1],
        )
        hidden = jnp.dot(normed, w_in, preferred_element_type=jnp.float32)
        hidden = jax.nn.gelu(hidden + ffn_bias[0], approximate=False).astype(jnp.bfloat16)
        encoded.append(
            settle(
                times_transposed(hidden, w_down),
                normed,
                shift[0, 2],
                norm_gain[0, 1],
                shift[0, 3],
            )
        )
    width = cross_weight.shape[3]
    own_part = lax.dynamic_slice_in_dim(
        jnp.concatenate(encoded, axis=0), lax.axis_index("row") * width, width, 1
    )
    outgoing = jnp.dot(chosen, own_part, preferred_element_type=jnp.float32)
    outgoing = outgoing.astype(jnp.bfloat16).reshape(n, capacity * PAGE, width)
    arrived = dispatch(outgoing).reshape(2, n * capacity * PAGE, width)
    pages = 16 if own_pages % 16 == 0 else own_pages
    cache = fill_cache(page_at, arrived, w_cross, pages)
    return (own_part, cache.transpose(0, 2, 1, 3))


def solution(mesh):
    return jax.shard_map(
        per_device,
        mesh=mesh,
        in_specs=(
            P("col", None),
            P("col"),
            P(None, "col", None, "row"),
            P(None, None, "row"),
            P(None, "row", "col"),
            P(None, "col", "row"),
            P(None, "row"),
            P(None, "row", "col"),
            P(),
            P(),
            P(None, "col", None, "row"),
            P("col", None),
            P(),
        ),
        out_specs=(P("col", "row"), P(None, "col", None, "row")),
        check_vma=False,
    )
```

time: 744 us -> 397 us (0.53)
  the two profiles are of different devices: /device:TPU:13 before, /device:TPU:25 now
where the time goes in v1:
time: 397 us; the launch traced here: 390 us
  waiting for transfers between devices  161 us (41%)
  Pallas kernels  111 us (28%)
  matrix products  43.2 us (11%)
  local copies, waits for them, and re-layouts  31.8 us (8%)
  other arithmetic  16.8 us (4%)
  between operations  15.1 us (4%)
  blocking collectives  8 us (2%)
    all_gather x5, waiting for transfers between devices, gather(): return lax.all_gather(value, 'col', axis=axis, tiled=True)  97.3 us
    pallas_call x1, Pallas kernels, dispatch(): pl.pallas_call(functools.partial(dispatch_kernel, n), in_specs=[pl.BlockS...  75 us
    ppermute x4, waiting for transfers between devices, settle(): theirs = lax.ppermute(mine, 'row', [(0, 1), (1, 0)])  61.2 us
    dot_general x4, matrix products, times_transposed(): lax.dot_general(left, right, (((1,), (1,)), ((), ())), preferred_element_...  39.5 us
    unnamed x35, local copies, waits for them, and re-layouts  30.5 us
    pallas_call x1, Pallas kernels, attention(): pl.pallas_call(functools.partial(attend_kernel, q_rows=256), grid=(width...  22.9 us
    pallas_call x1, Pallas kernels, fill_cache(): pl.pallas_call(functools.partial(cache_kernel, pages=pages), grid_spec=pl...  13 us
    unnamed x1, blocking collectives  8 us
  transfers between devices with their start and end apart: 9, of which 7 were waited for; matrix products, arithmetic and copies ran while one was open for 16% of the time, Pallas kernels for 25%

profile of v1, /device:TPU:25, one launch (start us, length us, event | category | flops | bytes accessed | tf_op | source)
XLA Modules:
  0.0 390.0 jit_solution(2372375572009340467)
XLA Ops:
  7.9 0.7 all-gather.10.cloned.1.call-update
  10.0 1.7 copy.27
  11.7 0.9 copy.22.seg_col_ref
  12.6 1.2 dynamic-slice
  14.5 41.1 %all-gather.8.cloned.1.call-done.w_ref = bf16[3,1024,512]{2,1,0:T(8,128)(2,1)} async-done(((bf16[3,64,512]{2,1,0:T(8,128)(2,1)}), bf16[3,1024,512]{2,1,0:T(8,128)(2,1)}) %all-gather.8.cloned.1.call-update) | async-done | bytes 3145744 | tf_op jit(solution)/shard_map/all_gather | solution.py:229
  55.6 1.6 copy-done
  57.2 0.7 copy-done.3
  57.9 1.9 copy-done.5
  60.5 22.9 %attention.1 = bf16[1024,512]{1,0:T(8,128)(2,1)S(1)} custom-call(bf16[1024,1024]{1,0:T(8,128)(2,1)S(1)} %copy-done, bf16[3,1024,512]{2,1,0:T(8,128)(2,1)S(1)} %copy-done.5, f32[2,512]{1,0:T(2,128)S(1)} %bitcast.64, s32[1024,1]{1,0:T(8,128)S(1)} %copy.22.seg_col_ref, s32[1,1024]{1,0:T(1,128)S(1)} %bitcast.63), custom_call_target="tpu_custom_call" | custom-call | flops 40000000000 | bytes 6291456 | tf_op jit(solution)/shard_map/attention/pallas_call | solution.py:62
  83.4 11.3 %all-gather.10.cloned.1.call-done = bf16[1024,512]{1,0:T(8,128)(2,1)} async-done(((bf16[64,512]{1,0:T(8,128)(2,1)}), bf16[1024,512]{1,0:T(8,128)(2,1)}) %all-gather.10.cloned.1.call-update) | async-done | bytes 1048592 | tf_op jit(solution)/shard_map/all_gather | solution.py:229
  94.7 2.9 convolution_convert_fusion.1
  97.6 1.2 collective-permute-start
  98.8 2.9 convolution_convert_fusion
  102.1 8.0 %all-reduce = s32[1024]{0:T(1024)S(1)} all-reduce(s32[1024]{0:T(1024)S(1)} %bitcast_dynamic-update-slice_fusion), channel_id=3, replica_groups=mesh['row'=2,'col'=16] {'col'}, use_global_device_ids=true, to_apply=%add | all-reduce | flops 1024 | bytes 8192
  111.8 10.6 %collective-permute-done = bf16[512,1024]{1,0:T(8,128)(2,1)} collective-permute-done((bf16[512,1024]{1,0:T(8,128)(2,1)}, bf16[512,1024]{1,0:T(8,128)(2,1)}, u32[]{:S(2)}, u32[]{:S(2)}) %collective-permute-start) | collective-permute-done | bytes 1048608 | tf_op jit(solution)/shard_map/ppermute | solution.py:191
  122.5 22.4 %collective-permute-done.2 = bf16[512,1024]{1,0:T(8,128)(2,1)S(1)} collective-permute-done((bf16[512,1024]{1,0:T(8,128)(2,1)}, bf16[512,1024]{1,0:T(8,128)(2,1)S(1)}, u32[]{:S(2)}, u32[]{:S(2)}) %collective-permute-start.2) | collective-permute-done | bytes 1048608 | tf_op jit(solution)/shard_map/ppermute | solution.py:191
  144.8 3.6 fusion.49
  148.5 4.0 %add_convert_fusion.3 = (bf16[512,1024]{1,0:T(8,128)(2,1)S(1)}, bf16[512,1024]{1,0:T(8,128)(2,1)}) fusion(f32[1024]{0:T(1024)S(1)} %bitcast.78, f32[1024]{0:T(1024)S(1)} %bitcast.76, f32[512]{0:T(512)S(1)} %get-tuple-element.38, f32[512]{0:T(512)S(1)} %get-tuple-element.39, f32[1024]{0:T(1024)S(1)} %bitcast.74, bf16[512,1024]{1,0:T(8,128)(2,1)} %collective-permute-done, ...), kind=kLoop, calls=%fused_computation.57 | loop fusion | flops 11534336 | bytes 8409088 | tf_op jit(solution)/shard_map/convert_element_type | solution.py:201
  152.5 44.9 %all-gather.12.cloned.1.call-done = bf16[1024,2048]{1,0:T(8,128)(2,1)} async-done(((bf16[64,2048]{1,0:T(8,128)(2,1)}), bf16[1024,2048]{1,0:T(8,128)(2,1)}) %all-gather.12.cloned.1.call-update) | async-done | bytes 4194320 | tf_op jit(solution)/shard_map/all_gather | solution.py:229
  197.4 16.8 %fusion.40 = bf16[512,1024]{1,0:T(8,128)(2,1)} fusion(bf16[1024,2048]{1,0:T(8,128)(2,1)} %all-gather.12.cloned.1.call-done, bf16[512,1024]{1,0:T(8,128)(2,1)} %get-tuple-element.21, bf16[1,1024,2048]{2,1,0:T(8,128)(2,1)} %all-gather.16.cloned.1.call-done, f32[2048]{0:T(1024)S(1)} %bitcast.82), kind=kOutput, calls=%fused_computation.63 | convolution fusion | flops 4364697600 | bytes 10493952 | tf_op jit(solution)/shard_map/dot_general | solution.py:205
  214.2 1.2 collective-permute-start.3
  215.4 16.8 %fusion.37 = bf16[512,1024]{1,0:T(8,128)(2,1)} fusion(bf16[1024,2048]{1,0:T(8,128)(2,1)} %all-gather.12.cloned.1.call-done, bf16[512,1024]{1,0:T(8,128)(2,1)S(1)} %get-tuple-element.20, bf16[1,1024,2048]{2,1,0:T(8,128)(2,1)} %all-gather.16.cloned.1.call-done, f32[2048]{0:T(1024)S(1)} %bitcast.83), kind=kOutput, calls=%fused_computation.62 | convolution fusion | flops 4364697600 | bytes 10493952 | tf_op jit(solution)/shard_map/dot_general | solution.py:205
  233.3 5.7 %collective-permute-done.3 = bf16[512,1024]{1,0:T(8,128)(2,1)} collective-permute-done((bf16[512,1024]{1,0:T(8,128)(2,1)}, bf16[512,1024]{1,0:T(8,128)(2,1)}, u32[]{:S(2)}, u32[]{:S(2)}) %collective-permute-start.3) | collective-permute-done | bytes 1048608 | tf_op jit(solution)/shard_map/ppermute | solution.py:191
  239.1 22.5 %collective-permute-done.1 = bf16[512,1024]{1,0:T(8,128)(2,1)} collective-permute-done((bf16[512,1024]{1,0:T(8,128)(2,1)}, bf16[512,1024]{1,0:T(8,128)(2,1)}, u32[]{:S(2)}, u32[]{:S(2)}) %collective-permute-start.1) | collective-permute-done | bytes 1048608 | tf_op jit(solution)/shard_map/ppermute | solution.py:191
  261.5 3.8 fusion.47
  265.3 3.1 add_convert_fusion
  268.6 3.7 fusion.30
  272.3 75.0 %dispatch.1 = bf16[2,16,128,512]{3,2,1,0:T(8,128)(2,1)} custom-call(bf16[16,128,512]{2,1,0:T(8,128)(2,1)} %bitcast.66), custom_call_target="tpu_custom_call" | custom-call | tf_op jit(solution)/shard_map/dispatch/pallas_call | solution.py:136
  347.4 2.2 copy-done.2
  349.5 2.2 copy-done.4
  351.7 13.0 %fill_cache.1 = bf16[2,2,2304,512]{3,2,1,0:T(8,128)(2,1)} custom-call(s32[144]{0:T(256)S(1)} %select_reduce_fusion.index_ref, bf16[2,2048,512]{2,1,0:T(8,128)(2,1)S(1)} %bitcast.61, bf16[2,2,1024,512]{3,2,1,0:T(8,128)(2,1)S(1)} %copy-done.4), custom_call_target="tpu_custom_call" | custom-call | flops 10000000000 | bytes 18874368 | tf_op jit(solution)/shard_map/fill_cache/pallas_call | solution.py:168
  364.8 18.3 %copy.25 = bf16[2,2304,2,512]{3,2,1,0:T(2,128)(2,1)} copy(bf16[2,2304,2,512]{3,1,2,0:T(8,128)(2,1)} %bitcast.65) | data formatting | bytes 18874368
  (63 shorter events, 6.1 us)
Async XLA Ops:
  7.2 48.5 %all-gather.8.cloned.1.call-start = ((), (), s32[]{:S(2)}) async-start(), calls=%async_computation | async-start | bytes 3342336 | tf_op jit(solution)/shard_map/all_gather | solution.py:229
  7.9 86.8 %all-gather.10.cloned.1.call-start = ((), (), s32[]{:S(2)}) async-start(), calls=%async_computation.1 | async-start | bytes 1114112 | tf_op jit(solution)/shard_map/all_gather | solution.py:229
  8.6 143.9 %all-gather.16.cloned.1.call-start = ((), (), s32[]{:S(2)}) async-start(), calls=%async_computation.4 | async-start | bytes 4456448 | tf_op jit(solution)/shard_map/all_gather | solution.py:229
  9.4 188.0 %all-gather.12.cloned.1.call-start = ((), (), s32[]{:S(2)}) async-start(), calls=%async_computation.2 | async-start | bytes 4456448 | tf_op jit(solution)/shard_map/all_gather | solution.py:229
  10.0 337.4 %all-gather.14.cloned.1.call-start = ((), (), s32[]{:S(2)}) async-start(), calls=%async_computation.3 | async-start | bytes 4456448 | tf_op jit(solution)/shard_map/all_gather | solution.py:229
  55.6 1.6 copy-start
  57.2 0.7 copy-start.3
  57.9 1.9 copy-start.5
  59.8 0.7 copy-start.6
  83.4 18.7 %copy-start.12 = (s32[64,1]{0,1:T(1,128)S(1)}, s32[64,1]{0,1:T(1,128)}, u32[]{:S(2)}) copy-start(s32[64,1]{0,1:T(1,128)} %param.24) | copy-start | bytes 772
  83.4 27.2 %copy-start.14 = (s32[16]{0:T(128)S(1)}, s32[16]{0:T(128)}, u32[]{:S(2)}) copy-start(s32[16]{0:T(128)} %param.25) | copy-start | bytes 196
  83.4 28.4 %copy-start.11 = (f32[1,2,1024]{2,1,0:T(2,128)S(1)}, f32[1,2,1024]{2,1,0:T(2,128)}, u32[]{:S(2)}) copy-start(f32[1,2,1024]{2,1,0:T(2,128)} %param.21) | copy-start | bytes 24580
  83.4 28.4 %copy-start.10 = (f32[1,4,1024]{2,1,0:T(4,128)S(1)}, f32[1,4,1024]{2,1,0:T(4,128)}, u32[]{:S(2)}) copy-start(f32[1,4,1024]{2,1,0:T(4,128)} %param.22) | copy-start | bytes 49156
  83.4 61.4 %copy-start.1 = (bf16[1024,1024]{1,0:T(8,128)(2,1)S(1)}, bf16[1024,1024]{1,0:T(8,128)(2,1)}, u32[]{:S(2)}) copy-start(bf16[1024,1024]{1,0:T(8,128)(2,1)} %x_ref.1) | copy-start | bytes 6291460
  97.6 24.8 %collective-permute-start = (bf16[512,1024]{1,0:T(8,128)(2,1)}, bf16[512,1024]{1,0:T(8,128)(2,1)}, u32[]{:S(2)}, u32[]{:S(2)}) collective-permute-start(bf16[512,1024]{1,0:T(8,128)(2,1)} %convolution_convert_fusion.1), channel_id=1, source_target_pairs={{0,16},{16,0},{1,17},{17,1},{2,18},{18,2},{3,19},{19,3},{4,20},{20... | collective-permute-start | bytes 3145736 | tf_op jit(solution)/shard_map/ppermute | solution.py:191
  101.8 43.1 %collective-permute-start.2 = (bf16[512,1024]{1,0:T(8,128)(2,1)}, bf16[512,1024]{1,0:T(8,128)(2,1)S(1)}, u32[]{:S(2)}, u32[]{:S(2)}) collective-permute-start(bf16[512,1024]{1,0:T(8,128)(2,1)} %convolution_convert_fusion), channel_id=1, source_target_pairs={{0,16},{16,0},{1,17},{17,1},{2,18},{18,2},{3,19},{19,3},{4,20},{20... | collective-permute-start | bytes 3145736 | tf_op jit(solution)/shard_map/ppermute | solution.py:191
  144.8 3.6 copy-start.8
  148.5 49.0 %copy-start.13 = (f32[1,2048]{1,0:T(1,128)S(1)}, f32[1,2048]{1,0:T(1,128)}, u32[]{:S(2)}) copy-start(f32[1,2048]{1,0:T(1,128)} %param.19) | copy-start | bytes 24580
  214.2 24.8 %collective-permute-start.3 = (bf16[512,1024]{1,0:T(8,128)(2,1)}, bf16[512,1024]{1,0:T(8,128)(2,1)}, u32[]{:S(2)}, u32[]{:S(2)}) collective-permute-start(bf16[512,1024]{1,0:T(8,128)(2,1)} %fusion.40), channel_id=1, source_target_pairs={{0,16},{16,0},{1,17},{17,1},{2,18},{18,2},{3,19},{19,3},{4,20},{20... | collective-permute-start | bytes 3145736 | tf_op jit(solution)/shard_map/ppermute | solution.py:191
  215.4 46.1 %copy-start.7 = (bf16[512,1024]{1,0:T(8,128)(2,1)S(1)}, bf16[512,1024]{1,0:T(8,128)(2,1)}, u32[]{:S(2)}) copy-start(bf16[512,1024]{1,0:T(8,128)(2,1)} %get-tuple-element.21) | copy-start | bytes 3145732
  232.2 29.3 %collective-permute-start.1 = (bf16[512,1024]{1,0:T(8,128)(2,1)}, bf16[512,1024]{1,0:T(8,128)(2,1)}, u32[]{:S(2)}, u32[]{:S(2)}) collective-permute-start(bf16[512,1024]{1,0:T(8,128)(2,1)} %fusion.37), channel_id=1, source_target_pairs={{0,16},{16,0},{1,17},{17,1},{2,18},{18,2},{3,19},{19,3},{4,20},{20... | collective-permute-start | bytes 3145736 | tf_op jit(solution)/shard_map/ppermute | solution.py:191
  268.6 3.7 copy-start.9
  347.3 2.2 copy-start.2
  349.5 2.2 copy-start.4
Sparse Core Ops, SparseCore 0:
  10.2 45.4 all-gather.7
  57.8 36.8 all-gather.9
  96.9 49.3 all-gather.15
  148.3 49.0 all-gather.11
  199.4 49.0 all-gather.13

commit v2 on v1

v2 whole, which is shorter than its diff:
```python
import functools

import jax
import jax.numpy as jnp
from jax import lax
from jax.experimental import pallas as pl
from jax.experimental.pallas import tpu as pltpu
from jax.sharding import PartitionSpec as P

HDIM = 64
PAGE = 16
BASE_MAX = 16
EPSILON = 1e-05
NEGATIVE = -1e30
CHUNKS = 4
MIB = 1 << 20
MESH = pl.DeviceIdType.MESH


def project_kernel(x_ref, w_ref, bias_ref, scale_ref, out_ref):
    sums = jnp.dot(x_ref[...], w_ref[0], preferred_element_type=jnp.float32)
    out_ref[0] = ((sums + bias_ref[0]) * scale_ref[0]).astype(jnp.bfloat16)


def project(tokens, weight, bias, scale):
    count, depth = tokens.shape
    width = weight.shape[2]
    return pl.pallas_call(
        project_kernel,
        grid=(3,),
        in_specs=[
            pl.BlockSpec((count, depth), lambda i: (0, 0)),
            pl.BlockSpec((1, depth, width), lambda i: (i, 0, 0)),
            pl.BlockSpec((1, 1, width), lambda i: (i, 0, 0)),
            pl.BlockSpec((1, 1, width), lambda i: (i, 0, 0)),
        ],
        out_specs=pl.BlockSpec((1, count, width), lambda i: (i, 0, 0)),
        out_shape=jax.ShapeDtypeStruct((3, count, width), jnp.bfloat16),
        compiler_params=pltpu.CompilerParams(vmem_limit_bytes=40 * MIB),
        cost_estimate=pl.CostEstimate(
            flops=5 * 10**9, bytes_accessed=8 * MIB, transcendentals=0
        ),
        name="project",
    )(tokens, weight, bias, scale)


def attend_kernel(q_ref, k_ref, v_ref, seg_col_ref, seg_row_ref, out_ref):
    allowed = seg_col_ref[...] == seg_row_ref[...]
    parts = []
    for h in range(q_ref.shape[2] // HDIM):
        cols = slice(h * HDIM, (h + 1) * HDIM)
        scores = lax.dot_general(
            q_ref[0, :, cols],
            k_ref[0, :, cols],
            (((1,), (1,)), ((), ())),
            preferred_element_type=jnp.float32,
        )
        scores = jnp.where(allowed, scores, NEGATIVE)
        highest = jnp.max(scores, axis=1, keepdims=True)
        exponent = jnp.exp(scores - highest)
        total = jnp.sum(exponent, axis=1, keepdims=True)
        mixed = jnp.dot(
            exponent.astype(jnp.bfloat16), v_ref[0, :, cols], preferred_element_type=jnp.float32
        )
        parts.append(mixed / total)
    out_ref[...] = jnp.concatenate(parts, axis=1).astype(jnp.bfloat16)


def attention(qkv, seg_col, seg_row, chunk, rows):
    _, count, width = qkv.shape
    step = 256
    return pl.pallas_call(
        attend_kernel,
        grid=(width // step,),
        in_specs=[
            pl.BlockSpec((1, rows, step), lambda i: (0, chunk, i)),
            pl.BlockSpec((1, count, step), lambda i: (1, 0, i)),
            pl.BlockSpec((1, count, step), lambda i: (2, 0, i)),
            pl.BlockSpec((rows, 1), lambda i: (chunk, 0)),
            pl.BlockSpec((1, count), lambda i: (0, 0)),
        ],
        out_specs=pl.BlockSpec((rows, step), lambda i: (0, i)),
        out_shape=jax.ShapeDtypeStruct((rows, width), jnp.bfloat16),
        compiler_params=pltpu.CompilerParams(vmem_limit_bytes=40 * MIB),
        cost_estimate=pl.CostEstimate(
            flops=5 * 10**9, bytes_accessed=3 * MIB, transcendentals=2 * MIB
        ),
        name="attention",
    )(qkv, qkv, qkv, seg_col, seg_row)


def feed_kernel(
    side_ref, mine_ref, theirs_ref, x_ref, vec_ref, w_ref, bias_ref,
    *rest,
):
    *part_refs, half_ref, normed_ref, sum_ref = rest
    step = pl.program_id(0)
    width = half_ref.shape[1]
    count = len(part_refs)

    def columns(at):
        at = at % count
        return slice(at * width, (at + 1) * width)

    @pl.when(step == 0)
    def _():
        summed = (
            x_ref[...].astype(jnp.float32)
            + (mine_ref[...].astype(jnp.float32) + theirs_ref[...].astype(jnp.float32))
            + vec_ref[0:1]
        )
        average = jnp.mean(summed, axis=1, keepdims=True)
        variance = jnp.mean(summed * summed, axis=1, keepdims=True) - average * average
        normed = (summed - average) * lax.rsqrt(variance + EPSILON) * vec_ref[1:2] + vec_ref[2:3]
        normed_ref[...] = normed.astype(jnp.bfloat16)
        sum_ref[...] = jnp.zeros_like(sum_ref)

        for side in range(count):

            @pl.when(side_ref[0] == side)
            def _():
                half_ref[...] = normed_ref[:, columns(side)]

    hidden = jnp.dot(normed_ref[...], w_ref[0], preferred_element_type=jnp.float32)
    hidden = hidden + bias_ref[...]
    hidden = (0.5 * hidden * (1.0 + lax.erf(hidden * 0.5**0.5))).astype(jnp.bfloat16)
    sum_ref[...] += lax.dot_general(
        hidden, w_ref[1], (((1,), (1,)), ((), ())), preferred_element_type=jnp.float32
    )

    @pl.when(step == pl.num_programs(0) - 1)
    def _():
        for side in range(count):

            @pl.when(side_ref[0] == side)
            def _():
                for k, part_ref in enumerate(part_refs):
                    part_ref[...] = sum_ref[:, columns(side + k)].astype(jnp.bfloat16)


def feed(side, mine, theirs, tokens, chunk, vectors, weight, bias):
    rows, depth = mine.shape
    count = lax.axis_size("row")
    width = depth // count
    units = weight.shape[2]
    step = 512
    whole = pl.BlockSpec((rows, depth), lambda i, s: (0, 0))
    half = pl.BlockSpec((rows, width), lambda i, s: (0, 0))
    return pl.pallas_call(
        feed_kernel,
        grid_spec=pltpu.PrefetchScalarGridSpec(
            num_scalar_prefetch=1,
            grid=(units // step,),
            in_specs=[
                whole,
                whole,
                pl.BlockSpec((rows, depth), lambda i, s: (chunk, 0)),
                pl.BlockSpec((3, depth), lambda i, s: (0, 0)),
                pl.BlockSpec((2, depth, step), lambda i, s: (0, 0, i)),
                pl.BlockSpec((1, step), lambda i, s: (0, i)),
            ],
            out_specs=[half] * (count + 1),
            scratch_shapes=[
                pltpu.VMEM((rows, depth), jnp.bfloat16),
                pltpu.VMEM((rows, depth), jnp.float32),
            ],
        ),
        out_shape=[jax.ShapeDtypeStruct((rows, width), jnp.bfloat16)] * (count + 1),
        compiler_params=pltpu.CompilerParams(vmem_limit_bytes=40 * MIB),
        cost_estimate=pl.CostEstimate(
            flops=8 * 10**9, bytes_accessed=10 * MIB, transcendentals=rows * units
        ),
        name="feed",
    )(side, mine, theirs, tokens, vectors, weight, bias)


def dispatch_kernel(
    n, sides, out_ref, got_ref, local_sem, send_sem, recv_sem, send2_sem, recv2_sem
):
    me, side = lax.axis_index("col"), lax.axis_index("row")
    barrier = pltpu.get_barrier_semaphore()
    for k in range(1, n):
        pl.semaphore_signal(
            barrier, inc=1, device_id=(side, lax.rem(me + k, n)), device_id_type=MESH
        )
    for j in range(1, sides):
        pl.semaphore_signal(
            barrier, inc=1, device_id=(lax.rem(side + j, sides), me), device_id_type=MESH
        )
    pl.semaphore_wait(barrier, n - 1 + sides - 1)

    def first(k):
        target = lax.rem(me + k, n)
        return pltpu.make_async_remote_copy(
            src_ref=out_ref.at[target],
            dst_ref=got_ref.at[side, me],
            send_sem=send_sem.at[k],
            recv_sem=recv_sem.at[k],
            device_id=(side, target),
            device_id_type=MESH,
        )

    def second(j, k, source):
        return pltpu.make_async_remote_copy(
            src_ref=source,
            dst_ref=got_ref.at[side, lax.rem(me + n - k, n)],
            send_sem=send2_sem.at[j, k],
            recv_sem=recv2_sem.at[j, k],
            device_id=(lax.rem(side + j, sides), me),
            device_id_type=MESH,
        )

    firsts = [first(k) for k in range(1, n)]
    for copy in firsts:
        copy.start()
    own = pltpu.make_async_copy(out_ref.at[me], got_ref.at[side, me], local_sem)
    own.start()
    seconds = [second(j, 0, out_ref.at[me]) for j in range(1, sides)]
    for copy in seconds:
        copy.start()
    for k in range(1, n):
        firsts[k - 1].wait_recv()
        for j in range(1, sides):
            copy = second(j, k, got_ref.at[side, lax.rem(me + n - k, n)])
            copy.start()
            seconds.append(copy)
    own.wait()
    for copy in firsts:
        copy.wait_send()
    for copy in seconds:
        copy.wait()


def dispatch(outgoing):
    n, rows, width = outgoing.shape
    sides = lax.axis_size("row")
    return pl.pallas_call(
        functools.partial(dispatch_kernel, n, sides),
        in_specs=[pl.BlockSpec(memory_space=pl.ANY)],
        out_specs=pl.BlockSpec(memory_space=pl.ANY),
        out_shape=jax.ShapeDtypeStruct((sides, n, rows, width), outgoing.dtype),
        scratch_shapes=[pltpu.SemaphoreType.DMA(())]
        + [pltpu.SemaphoreType.DMA((n,))] * 2
        + [pltpu.SemaphoreType.DMA((sides, n))] * 2,
        compiler_params=pltpu.CompilerParams(collective_id=1, has_side_effects=True),
        name="dispatch",
    )(outgoing)


def cache_kernel(index_ref, got_ref, w_ref, out_ref, x_ref, *, pages):
    base = pl.program_id(0) * pages
    half = got_ref.shape[2]
    for j in range(pages):
        at = index_ref[base + j]
        rows = pl.ds(pl.multiple_of(jnp.maximum(at, 0) * PAGE, PAGE), PAGE)
        for s in range(got_ref.shape[0]):
            page = got_ref[s, rows, :]
            page = jnp.where(at >= 0, page, jnp.zeros_like(page))
            x_ref[j * PAGE : (j + 1) * PAGE, s * half : (s + 1) * half] = page
    x = x_ref[...]
    for d in range(w_ref.shape[0]):
        pair = [
            jnp.dot(x, w_ref[d, k], preferred_element_type=jnp.float32).astype(jnp.bfloat16)
            for k in range(2)
        ]
        out_ref[d] = jnp.stack(pair, axis=1)


def fill_cache(index, got, weight, pages):
    own_pages = index.shape[0]
    layers, _, depth, width = weight.shape
    return pl.pallas_call(
        functools.partial(cache_kernel, pages=pages),
        grid_spec=pltpu.PrefetchScalarGridSpec(
            num_scalar_prefetch=1,
            grid=(own_pages // pages,),
            in_specs=[
                pl.BlockSpec(got.shape, lambda i, s: (0, 0, 0)),
                pl.BlockSpec(weight.shape, lambda i, s: (0, 0, 0, 0)),
            ],
            out_specs=pl.BlockSpec((layers, pages * PAGE, 2, width), lambda i, s: (0, i, 0, 0)),
            scratch_shapes=[pltpu.VMEM((pages * PAGE, depth), jnp.bfloat16)],
        ),
        out_shape=jax.ShapeDtypeStruct((layers, own_pages * PAGE, 2, width), jnp.bfloat16),
        compiler_params=pltpu.CompilerParams(vmem_limit_bytes=40 * MIB),
        cost_estimate=pl.CostEstimate(
            flops=10**10, bytes_accessed=18 * MIB, transcendentals=0
        ),
        name="fill_cache",
    )(index, got, weight)


def send(value, step):
    count = lax.axis_size("row")
    return lax.ppermute(value, "row", [(i, (i + step) % count) for i in range(count)])


def from_others(values):
    got = [send(value, k + 1) for k, value in enumerate(values)]
    if len(got) == 1:
        return got[0]
    return sum(value.astype(jnp.float32) for value in got)


def times_transposed(left, right):
    return lax.dot_general(
        left, right, (((1,), (1,)), ((), ())), preferred_element_type=jnp.float32
    )


def per_device(
    tokens,
    segment_ids,
    qkv_weight,
    attn_bias,
    out_weight,
    ffn_in,
    ffn_bias,
    ffn_out,
    norm_gain,
    shift,
    cross_weight,
    page_owner,
    cache_base,
):
    token_count = tokens.shape[0]
    n, me = lax.axis_size("col"), lax.axis_index("col")

    def gather(value, axis):
        return lax.all_gather(value, "col", axis=axis, tiled=True)

    w_first = gather(
        jnp.concatenate([qkv_weight[0].transpose(1, 0, 2), out_weight.transpose(0, 2, 1)]), 1
    )
    w_ffn = gather(jnp.concatenate([ffn_in, ffn_out.transpose(0, 2, 1)]), 1)
    w_cross = gather(cross_weight.transpose(0, 2, 1, 3), 2)
    all_owners = lax.all_gather(page_owner[:, 0], "col")

    page_count = page_owner.shape[0]
    capacity = max(2, (2 * page_count + n - 1) // n)
    owner_ids = jnp.arange(n, dtype=jnp.int32)
    owners = page_owner[:, 0]
    onehot = (owners[:, None] == owner_ids[None, :]).astype(jnp.int32)
    local_rank = jnp.sum((jnp.cumsum(onehot, axis=0) - onehot) * onehot, axis=1)
    target = owners * capacity + local_rank
    token_target = (
        target[:, None] * PAGE + jnp.arange(PAGE, dtype=jnp.int32)[None, :]
    ).reshape(token_count)
    received = jnp.sum((all_owners == me).astype(jnp.int32), axis=1)
    earlier = jnp.cumsum(received) - received
    own_base = jnp.sum(jnp.where(owner_ids == me, cache_base, 0))
    place_ids = jnp.arange(capacity, dtype=jnp.int32)
    slots = jnp.where(
        place_ids[None, :] < received[:, None],
        own_base + earlier[:, None] + place_ids[None, :],
        -1,
    ).reshape(n * capacity)
    own_pages = BASE_MAX + capacity * n
    hits = jnp.arange(own_pages, dtype=jnp.int32)[:, None] == slots[None, :]
    page_at = jnp.max(
        jnp.where(hits, jnp.arange(n * capacity, dtype=jnp.int32)[None, :], -1), axis=1
    )

    page_at, token_target, tokens = lax.optimization_barrier((page_at, token_target, tokens))
    width = cross_weight.shape[3]
    side = lax.axis_index("row")
    others = lax.axis_size("row") - 1
    bias = jnp.stack([attn_bias[0, 0], jnp.zeros_like(attn_bias[0, 0]), attn_bias[0, 1]])
    scale = jnp.array([HDIM ** (-0.5), 1.0, 1.0], jnp.float32)[:, None, None]
    scale = jnp.broadcast_to(scale, (3, 1, bias.shape[1]))
    qkv = project(tokens, w_first, bias[:, None, :], scale)
    w_out = w_first[3]
    vectors = jnp.stack([shift[0, 0], norm_gain[0, 0], shift[0, 1]])
    rows = token_count // CHUNKS
    seg_col, seg_row = segment_ids[:, None], segment_ids[None, :]
    partials = []
    for c in range(CHUNKS):
        context = attention(qkv, seg_col, seg_row, c, rows)
        mine = times_transposed(context, w_out).astype(jnp.bfloat16)
        partials.append((mine, from_others([mine] * others)))
    kept, taken, halves = [], [], []
    for c, (mine, theirs) in enumerate(partials):
        keep, *sends, half = feed(
            side.reshape(1), mine, theirs, tokens, c, vectors, w_ffn, ffn_bias
        )
        kept.append(keep)
        taken.append(from_others(sends))
        halves.append(half)

    def own(row):
        return lax.dynamic_slice_in_dim(row, side * width, width, 0)

    summed = (
        jnp.concatenate(halves).astype(jnp.float32)
        + (jnp.concatenate(kept).astype(jnp.float32) + jnp.concatenate(taken).astype(jnp.float32))
        + own(shift[0, 2])
    )
    sums = jnp.stack([jnp.sum(summed, axis=1), jnp.sum(summed * summed, axis=1)])
    moments = (sums + from_others([sums] * others)) / tokens.shape[1]
    average = moments[0][:, None]
    variance = moments[1][:, None] - average * average
    own_part = (
        (summed - average) * lax.rsqrt(variance + EPSILON) * own(norm_gain[0, 1])
        + own(shift[0, 3])
    ).astype(jnp.bfloat16)
    chosen = (
        jnp.arange(n * capacity * PAGE, dtype=jnp.int32)[:, None] == token_target[None, :]
    ).astype(jnp.bfloat16)
    outgoing = jnp.dot(chosen, own_part, preferred_element_type=jnp.float32)
    outgoing = outgoing.astype(jnp.bfloat16).reshape(n, capacity * PAGE, width)
    arrived = dispatch(outgoing).reshape(others + 1, n * capacity * PAGE, width)
    pages = 16 if own_pages % 16 == 0 else own_pages
    cache = fill_cache(page_at, arrived, w_cross, pages)
    return (own_part, cache)


def solution(mesh):
    return jax.shard_map(
        per_device,
        mesh=mesh,
        in_specs=(
            P("col", None),
            P("col"),
            P(None, "col", None, "row"),
            P(None, None, "row"),
            P(None, "row", "col"),
            P(None, "col", "row"),
            P(None, "row"),
            P(None, "row", "col"),
            P(),
            P(),
            P(None, "col", None, "row"),
            P("col", None),
            P(),
        ),
        out_specs=(P("col", "row"), P(None, "col", None, "row")),
        check_vma=False,
    )
```

time: 397 us -> 300 us (0.76); the launches traced: 390 us -> 300 us
  waiting for transfers between devices: 161 us -> 89.5 us
  Pallas kernels: 111 us -> 148 us
  matrix products: 43.2 us -> 6.4 us
  local copies, waits for them, and re-layouts: 31.8 us -> 20.1 us
  other arithmetic: 16.8 us -> 8.3 us
    ppermute x4 -> x9, waiting for transfers between devices: 61.2 us -> 9.4 us  [send(): lax.ppermute(value, 'row', [(i, (i + step) % count) for i in range(count)])]
    dot_general x4, matrix products: 39.5 us -> 2.74 us  [times_transposed(): lax.dot_general(left, right, (((1,), (1,)), ((), ())), preferred_element_...]
    pallas_call x2 -> x10, Pallas kernels: 97.9 us -> 122 us  [the longest x1 76 us: dispatch(): pl.pallas_call(functools.partial(dispatch_kernel, n, sides), in_specs=[pl...]
    all_gather x5 -> x3, waiting for transfers between devices: 97.3 us -> 80 us  [gather(): return lax.all_gather(value, 'col', axis=axis, tiled=True)]
    pallas_call x1, Pallas kernels: 13 us -> 26.1 us  [fill_cache(): pl.pallas_call(functools.partial(cache_kernel, pages=pages), grid_spec=pl...]
    unnamed x35 -> x54, local copies, waits for them, and re-layouts: 30.5 us -> 19.3 us
    convert_element_type x2 -> x1, other arithmetic: 7.18 us -> 0.39 us  [per_device(): own_part = ((summed - average) * lax.rsqrt(variance + EPSILON) * own(norm...]
    reduce_sum x2 -> x1, other arithmetic: 7.37 us -> 1.96 us  [per_device(): jnp.sum(summed, axis=1)]
  transfers between devices with their start and end apart: 9 -> 12, of which waited for: 7 -> 5; matrix products, arithmetic and copies ran while one was open for 16% -> 5% of each run, Pallas kernels for 25% -> 41%
where the time goes in v2:
time: 300 us
  Pallas kernels  148 us (49%)
  waiting for transfers between devices  89.5 us (30%)
  local copies, waits for them, and re-layouts  20.1 us (7%)
  between operations  14.8 us (5%)
  other arithmetic  8.3 us (3%)
  starting transfers between devices  6.57 us (2%)
  blocking collectives  6.49 us (2%)
  matrix products  6.4 us (2%)
    all_gather x3, waiting for transfers between devices, gather(): return lax.all_gather(value, 'col', axis=axis, tiled=True)  80 us
    pallas_call x1, Pallas kernels, dispatch(): pl.pallas_call(functools.partial(dispatch_kernel, n, sides), in_specs=[pl...  76 us
    pallas_call x1, Pallas kernels, fill_cache(): pl.pallas_call(functools.partial(cache_kernel, pages=pages), grid_spec=pl...  26.1 us
    pallas_call x4, Pallas kernels, feed(): pl.pallas_call(feed_kernel, grid_spec=pltpu.PrefetchScalarGridSpec(num_sc...  22 us
    pallas_call x4, Pallas kernels, attention(): pl.pallas_call(attend_kernel, grid=(width // step,), in_specs=[pl.BlockSp...  19.8 us
    unnamed x54, local copies, waits for them, and re-layouts  19.3 us
    ppermute x9, waiting for transfers between devices, send(): lax.ppermute(value, 'row', [(i, (i + step) % count) for i in range(count)])  9.4 us
    unnamed x1, blocking collectives  6.49 us
  transfers between devices with their start and end apart: 12, of which 5 were waited for; matrix products, arithmetic and copies ran while one was open for 5% of the time, Pallas kernels for 41%

profile of v2, /device:TPU:25, one launch (start us, length us, event | category | flops | bytes accessed | tf_op | source)
XLA Modules:
  0.0 299.8 jit_solution(18173944577758590989)
XLA Ops:
  7.3 1.8 pad_maximum_fusion.1
  9.1 1.9 pad_maximum_fusion
  13.3 6.5 %all-reduce = s32[1024]{0:T(1024)S(1)} all-reduce(s32[1024]{0:T(1024)S(1)} %bitcast_dynamic-update-slice_fusion), channel_id=2, replica_groups=mesh['row'=2,'col'=16] {'col'}, use_global_device_ids=true, to_apply=%add | all-reduce | flops 1024 | bytes 8192
  22.8 38.8 %all-gather.5.cloned.1.call-done.w_ref = bf16[4,1024,512]{2,1,0:T(8,128)(2,1)} async-done(((bf16[4,64,512]{2,1,0:T(8,128)(2,1)}), bf16[4,1024,512]{2,1,0:T(8,128)(2,1)}) %all-gather.5.cloned.1.call-update) | async-done | bytes 4194320 | tf_op jit(solution)/shard_map/all_gather | solution.py:330
  61.7 2.2 copy-done.5
  63.9 1.6 copy-done.7
  65.4 3.8 %project.1.q_ref.k_ref.v_ref = bf16[3,1024,512]{2,1,0:T(8,128)(2,1)S(1)} custom-call(bf16[1024,1024]{1,0:T(8,128)(2,1)S(1)} %copy-done.7, bf16[4,1024,512]{2,1,0:T(8,128)(2,1)S(1)} %copy-done.5, f32[3,1,512]{2,1,0:T(1,128)S(1)} %broadcast_in_dim.32.bias_ref, f32[3,1,512]{2,1,0:T(1,128)S(1)} %broadcast_in_dim.54.scale_ref), custom_call_target="tpu_custom_call" | custom-call | flops 5000000000 | bytes 8388608 | tf_op jit(solution)/shard_map/project/pallas_call | solution.py:28
  69.2 5.0 %attention.7 = bf16[256,512]{1,0:T(8,128)(2,1)S(1)} custom-call(bf16[3,1024,512]{2,1,0:T(8,128)(2,1)S(1)} %project.1.q_ref.k_ref.v_ref, bf16[3,1024,512]{2,1,0:T(8,128)(2,1)S(1)} %project.1.q_ref.k_ref.v_ref, bf16[3,1024,512]{2,1,0:T(8,128)(2,1)S(1)} %project.1.q_ref.k_ref.v_ref, s32[1024,1]{1,0:T(8,128)S(1)} %copy.25.seg_col_ref, s32[1,1024]{1,0:T(1,128)S(1)} %bitcast.56), custom_call_target="tpu_custom_call" | custom-call | flops 5000000000 | bytes 3145728 | tf_op jit(solution)/shard_map/attention/pallas_call | solution.py:72
  74.7 1.2 collective-permute-start.3
  76.0 5.0 %attention.6 = bf16[256,512]{1,0:T(8,128)(2,1)S(1)} custom-call(bf16[3,1024,512]{2,1,0:T(8,128)(2,1)S(1)} %project.1.q_ref.k_ref.v_ref, bf16[3,1024,512]{2,1,0:T(8,128)(2,1)S(1)} %project.1.q_ref.k_ref.v_ref, bf16[3,1024,512]{2,1,0:T(8,128)(2,1)S(1)} %project.1.q_ref.k_ref.v_ref, s32[1024,1]{1,0:T(8,128)S(1)} %copy.25.seg_col_ref, s32[1,1024]{1,0:T(1,128)S(1)} %bitcast.57), custom_call_target="tpu_custom_call" | custom-call | flops 5000000000 | bytes 3145728 | tf_op jit(solution)/shard_map/attention/pallas_call | solution.py:72
  80.9 1.3 convolution_convert_fusion.1.mine_ref
  82.6 5.0 %attention.5 = bf16[256,512]{1,0:T(8,128)(2,1)S(1)} custom-call(bf16[3,1024,512]{2,1,0:T(8,128)(2,1)S(1)} %project.1.q_ref.k_ref.v_ref, bf16[3,1024,512]{2,1,0:T(8,128)(2,1)S(1)} %project.1.q_ref.k_ref.v_ref, bf16[3,1024,512]{2,1,0:T(8,128)(2,1)S(1)} %project.1.q_ref.k_ref.v_ref, s32[1024,1]{1,0:T(8,128)S(1)} %copy.25.seg_col_ref, s32[1,1024]{1,0:T(1,128)S(1)} %bitcast.58), custom_call_target="tpu_custom_call" | custom-call | flops 5000000000 | bytes 3145728 | tf_op jit(solution)/shard_map/attention/pallas_call | solution.py:72
  88.0 1.3 collective-permute-start.1
  89.3 5.0 %attention.4 = bf16[256,512]{1,0:T(8,128)(2,1)S(1)} custom-call(bf16[3,1024,512]{2,1,0:T(8,128)(2,1)S(1)} %project.1.q_ref.k_ref.v_ref, bf16[3,1024,512]{2,1,0:T(8,128)(2,1)S(1)} %project.1.q_ref.k_ref.v_ref, bf16[3,1024,512]{2,1,0:T(8,128)(2,1)S(1)} %project.1.q_ref.k_ref.v_ref, s32[1024,1]{1,0:T(8,128)S(1)} %copy.25.seg_col_ref, s32[1,1024]{1,0:T(1,128)S(1)} %bitcast.59), custom_call_target="tpu_custom_call" | custom-call | flops 5000000000 | bytes 3145728 | tf_op jit(solution)/shard_map/attention/pallas_call | solution.py:72
  95.8 41.2 %all-gather.7.cloned.1.call-done.w_ref = bf16[2,1024,2048]{2,1,0:T(8,128)(2,1)} async-done(((bf16[2,64,2048]{2,1,0:T(8,128)(2,1)}), bf16[2,1024,2048]{2,1,0:T(8,128)(2,1)}) %all-gather.7.cloned.1.call-update) | async-done | bytes 8388624 | tf_op jit(solution)/shard_map/all_gather | solution.py:330
  137.0 3.4 %copy-done.2 = bf16[2,1024,2048]{2,1,0:T(8,128)(2,1)S(1)} copy-done((bf16[2,1024,2048]{2,1,0:T(8,128)(2,1)S(1)}, bf16[2,1024,2048]{2,1,0:T(8,128)(2,1)}, u32[]{:S(2)}) %copy-start.2) | copy-done | bytes 8388632
  140.4 1.6 copy-done.8
  142.0 1.0 copy-done.12
  144.1 4.7 %feed.7 = (bf16[256,512]{1,0:T(8,128)(2,1)S(1)}, bf16[256,512]{1,0:T(8,128)(2,1)S(1)}, bf16[256,512]{1,0:T(8,128)(2,1)S(1)}) custom-call(s32[1]{0:T(128)} %bitcast.side_ref, bf16[256,1024]{1,0:T(8,128)(2,1)S(1)} %copy-done.12, bf16[256,1024]{1,0:T(8,128)(2,1)S(1)} %copy-done.14, bf16[1024,1024]{1,0:T(8,128)(2,1)S(1)} %copy-done.8, ...), custom_call_target="tpu_custom_call" | custom-call | flops 8000000000 | bytes 10485760 | tf_op jit(solution)/shard_map/feed/pallas_call | solution.py:149
  148.8 1.3 collective-permute-start.7
  150.1 6.4 %feed.6 = (bf16[256,512]{1,0:T(8,128)(2,1)S(1)}, bf16[256,512]{1,0:T(8,128)(2,1)}, bf16[256,512]{1,0:T(8,128)(2,1)S(1)}) custom-call(s32[1]{0:T(128)} %bitcast.side_ref, bf16[256,1024]{1,0:T(8,128)(2,1)} %convolution_convert_fusion.1.mine_ref, bf16[256,1024]{1,0:T(8,128)(2,1)} %collective-permute-done.2.theirs_ref, bf16[1024,1024]{1,0:T(8,128)(2,1)S(1)} %copy-done.8, ...), custom_call_target="tpu_custom_call" | custom-call | flops 8000000000 | bytes 10485760 | tf_op jit(solution)/shard_map/feed/pallas_call | solution.py:149
  158.6 5.4 %feed.5 = (bf16[256,512]{1,0:T(8,128)(2,1)S(1)}, bf16[256,512]{1,0:T(8,128)(2,1)}, bf16[256,512]{1,0:T(8,128)(2,1)S(1)}) custom-call(s32[1]{0:T(128)} %bitcast.side_ref, bf16[256,1024]{1,0:T(8,128)(2,1)S(1)} %convolution_convert_fusion.2.mine_ref, bf16[256,1024]{1,0:T(8,128)(2,1)S(1)} %copy-done.10, bf16[1024,1024]{1,0:T(8,128)(2,1)S(1)} %copy-done.8, ...), custom_call_target="tpu_custom_call" | custom-call | flops 8000000000 | bytes 10485760 | tf_op jit(solution)/shard_map/feed/pallas_call | solution.py:149
  164.0 1.2 collective-permute-start.5
  165.3 5.4 %feed.4 = (bf16[256,512]{1,0:T(8,128)(2,1)S(1)}, bf16[256,512]{1,0:T(8,128)(2,1)}, bf16[256,512]{1,0:T(8,128)(2,1)S(1)}) custom-call(s32[1]{0:T(128)} %bitcast.side_ref, bf16[256,1024]{1,0:T(8,128)(2,1)S(1)} %convolution_convert_fusion.3.mine_ref, bf16[256,1024]{1,0:T(8,128)(2,1)S(1)} %collective-permute-done.theirs_ref, bf16[1024,1024]{1,0:T(8,128)(2,1)S(1)} %copy-done.8, ...), custom_call_target="tpu_custom_call" | custom-call | flops 8000000000 | bytes 10485760 | tf_op jit(solution)/shard_map/feed/pallas_call | solution.py:149
  171.4 6.3 %collective-permute-done.4 = bf16[256,512]{1,0:T(8,128)(2,1)S(1)} collective-permute-done((bf16[256,512]{1,0:T(8,128)(2,1)}, bf16[256,512]{1,0:T(8,128)(2,1)S(1)}, u32[]{:S(2)}, u32[]{:S(2)}) %collective-permute-start.4) | collective-permute-done | bytes 262176 | tf_op jit(solution)/shard_map/ppermute | solution.py:295
  177.7 2.0 fusion.7
  180.0 2.6 collective-permute-done.8
  183.1 3.7 %fusion.2 = bf16[2048,512]{1,0:T(8,128)(2,1)} fusion(bf16[1024,512]{1,0:T(8,128)(2,1)S(1)} %add_convert_fusion, s32[1024]{0:T(1024)S(1)} %add.101), kind=kOutput, calls=%fused_computation.3 | convolution fusion | flops 2150629376 | bytes 3149824 | tf_op jit(solution)/shard_map/dot_general | solution.py:409
  186.8 76.0 %dispatch.1 = bf16[2,16,128,512]{3,2,1,0:T(8,128)(2,1)} custom-call(bf16[16,128,512]{2,1,0:T(8,128)(2,1)} %bitcast.60), custom_call_target="tpu_custom_call" | custom-call | tf_op jit(solution)/shard_map/dispatch/pallas_call | solution.py:237
  262.8 2.2 copy-done
  265.0 2.2 copy-done.4
  267.2 26.1 %fill_cache.1 = bf16[2,2304,2,512]{3,2,1,0:T(2,128)(2,1)} custom-call(s32[144]{0:T(256)S(1)} %select_reduce_fusion.index_ref, bf16[2,2048,512]{2,1,0:T(8,128)(2,1)S(1)} %bitcast.54, bf16[2,2,1024,512]{3,2,1,0:T(8,128)(2,1)S(1)} %copy-done.4), custom_call_target="tpu_custom_call" | custom-call | flops 10000000000 | bytes 18874368 | tf_op jit(solution)/shard_map/fill_cache/pallas_call | solution.py:272
  (102 shorter events, 12.2 us)
Async XLA Ops:
  7.2 4.7 %copy-start.24 = (u32[32]{0:T(128)S(1)}, u32[32]{0:T(128)}, u32[]{:S(2)}) copy-start(u32[32]{0:T(128)} %constant.46) | copy-start | bytes 388
  7.2 54.4 %copy-start.22 = (f32[3]{0:T(128)S(1)}, f32[3]{0:T(128)}, u32[]{:S(2)}) copy-start(f32[3]{0:T(128)} %constant.43.clone) | copy-start | bytes 40
  7.2 3.9 %copy-start.17 = (bf16[2,64,2,512]{3,2,1,0:T(2,128)(2,1)S(1)}, bf16[2,64,2,512]{3,2,1,0:T(2,128)(2,1)}, u32[]{:S(2)}) copy-start(bf16[2,64,2,512]{3,2,1,0:T(2,128)(2,1)} %param.24) | copy-start | bytes 786436
  7.2 4.7 %copy-start.18 = (f32[1,4,1024]{2,1,0:T(4,128)S(1)}, f32[1,4,1024]{2,1,0:T(4,128)}, u32[]{:S(2)}) copy-start(f32[1,4,1024]{2,1,0:T(4,128)} %param.23) | copy-start | bytes 49156
  7.2 5.9 %copy-start.21 = (s32[64,1]{0,1:T(1,128)S(1)}, s32[64,1]{0,1:T(1,128)}, u32[]{:S(2)}) copy-start(s32[64,1]{0,1:T(1,128)} %param.25) | copy-start | bytes 772
  7.2 13.0 %copy-start.23 = (s32[16]{0:T(128)S(1)}, s32[16]{0:T(128)}, u32[]{:S(2)}) copy-start(s32[16]{0:T(128)} %param.26) | copy-start | bytes 196
  7.2 15.1 %copy-start.20 = (f32[1,2,512]{2,1,0:T(2,128)S(1)}, f32[1,2,512]{2,1,0:T(2,128)}, u32[]{:S(2)}) copy-start(f32[1,2,512]{2,1,0:T(2,128)} %param.17) | copy-start | bytes 12292
  7.2 15.3 %copy-start.1 = (s32[1024]{0:T(1024)S(1)}, s32[1024]{0:T(1024)}, u32[]{:S(2)}) copy-start(s32[1024]{0:T(1024)} %param.15) | copy-start | bytes 12292
  7.3 15.5 %copy-start.19 = (f32[1,2,1024]{2,1,0:T(2,128)S(1)}, f32[1,2,1024]{2,1,0:T(2,128)}, u32[]{:S(2)}) copy-start(f32[1,2,1024]{2,1,0:T(2,128)} %param.22) | copy-start | bytes 24580
  7.3 54.3 %all-gather.5.cloned.1.call-start = ((), (), s32[]{:S(2)}) async-start(), calls=%async_computation | async-start | bytes 4456448 | tf_op jit(solution)/shard_map/all_gather | solution.py:330
  9.1 127.9 %all-gather.7.cloned.1.call-start = ((), (), s32[]{:S(2)}) async-start(), calls=%async_computation.1 | async-start | bytes 8912896 | tf_op jit(solution)/shard_map/all_gather | solution.py:330
  11.0 251.8 %all-gather.9.cloned.1.call-start = ((), (), s32[]{:S(2)}) async-start(), calls=%async_computation.2 | async-start | bytes 4456448 | tf_op jit(solution)/shard_map/all_gather | solution.py:330
  61.7 2.2 copy-start.5
  63.8 1.6 copy-start.7
  69.2 5.0 %copy-start.6 = (bf16[4,1024,512]{2,1,0:T(8,128)(2,1)S(1)}, bf16[4,1024,512]{2,1,0:T(8,128)(2,1)}, u32[]{:S(2)}) copy-start(bf16[4,1024,512]{2,1,0:T(8,128)(2,1)} %all-gather.5.cloned.1.call-done.w_ref) | copy-start | bytes 12582916
  74.7 6.2 %copy-start.11 = (bf16[256,1024]{1,0:T(8,128)(2,1)}, bf16[256,1024]{1,0:T(8,128)(2,1)S(1)}, u32[]{:S(2)}) copy-start(bf16[256,1024]{1,0:T(8,128)(2,1)S(1)} %convolution_convert_fusion.mine_ref) | copy-start | bytes 1572868
  74.7 20.3 %collective-permute-start.3 = (bf16[256,1024]{1,0:T(8,128)(2,1)S(1)}, bf16[256,1024]{1,0:T(8,128)(2,1)S(1)}, u32[]{:S(2)}, u32[]{:S(2)}) collective-permute-start(bf16[256,1024]{1,0:T(8,128)(2,1)S(1)} %convolution_convert_fusion.mine_ref), channel_id=1, source_target_pairs={{0,16},{16,0},{1,17},{17,1},{2,18},{18,2},{3,19},{19,3},{4,20},{20... | collective-permute-start | bytes 1572872 | tf_op jit(solution)/shard_map/ppermute | solution.py:295
  82.3 67.8 %collective-permute-start.2 = (bf16[256,1024]{1,0:T(8,128)(2,1)}, bf16[256,1024]{1,0:T(8,128)(2,1)}, u32[]{:S(2)}, u32[]{:S(2)}) collective-permute-start(bf16[256,1024]{1,0:T(8,128)(2,1)} %convolution_convert_fusion.1.mine_ref), channel_id=1, source_target_pairs={{0,16},{16,0},{1,17},{17,1},{2,18},{18,2},{3,19},{19,3},{4,20},{20... | collective-permute-start | bytes 1572872 | tf_op jit(solution)/shard_map/ppermute | solution.py:295
  88.0 49.0 %copy-start.15 = (f32[1,2048]{1,0:T(1,128)S(1)}, f32[1,2048]{1,0:T(1,128)}, u32[]{:S(2)}) copy-start(f32[1,2048]{1,0:T(1,128)} %bias_ref.7) | copy-start | bytes 24580
  88.0 68.8 %collective-permute-start.1 = (bf16[256,1024]{1,0:T(8,128)(2,1)S(1)}, bf16[256,1024]{1,0:T(8,128)(2,1)S(1)}, u32[]{:S(2)}, u32[]{:S(2)}) collective-permute-start(bf16[256,1024]{1,0:T(8,128)(2,1)S(1)} %convolution_convert_fusion.2.mine_ref), channel_id=1, source_target_pairs={{0,16},{16,0},{1,17},{17,1},{2,18},{18,2},{3,19},{19,3},{4,20},{20... | collective-permute-start | bytes 1572872 | tf_op jit(solution)/shard_map/ppermute | solution.py:295
  94.7 70.5 %collective-permute-start = (bf16[256,1024]{1,0:T(8,128)(2,1)S(1)}, bf16[256,1024]{1,0:T(8,128)(2,1)S(1)}, u32[]{:S(2)}, u32[]{:S(2)}) collective-permute-start(bf16[256,1024]{1,0:T(8,128)(2,1)S(1)} %convolution_convert_fusion.3.mine_ref), channel_id=1, source_target_pairs={{0,16},{16,0},{1,17},{17,1},{2,18},{18,2},{3,19},{19,3},{4,20},{20... | collective-permute-start | bytes 1572872 | tf_op jit(solution)/shard_map/ppermute | solution.py:295
  137.0 3.4 %copy-start.2 = (bf16[2,1024,2048]{2,1,0:T(8,128)(2,1)S(1)}, bf16[2,1024,2048]{2,1,0:T(8,128)(2,1)}, u32[]{:S(2)}) copy-start(bf16[2,1024,2048]{2,1,0:T(8,128)(2,1)} %all-gather.7.cloned.1.call-done.w_ref) | copy-start | bytes 25165828
  140.4 1.6 copy-start.8
  144.1 6.0 %copy-start.3 = (bf16[2,1024,2048]{2,1,0:T(8,128)(2,1)S(1)}, bf16[2,1024,2048]{2,1,0:T(8,128)(2,1)}, u32[]{:S(2)}) copy-start(bf16[2,1024,2048]{2,1,0:T(8,128)(2,1)} %all-gather.7.cloned.1.call-done.w_ref) | copy-start | bytes 25165828
  148.8 22.1 %collective-permute-start.7 = (bf16[256,512]{1,0:T(8,128)(2,1)S(1)}, bf16[256,512]{1,0:T(8,128)(2,1)}, u32[]{:S(2)}, u32[]{:S(2)}) collective-permute-start(bf16[256,512]{1,0:T(8,128)(2,1)S(1)} %get-tuple-element.29), channel_id=1, source_target_pairs={{0,16},{16,0},{1,17},{17,1},{2,18},{18,2},{3,19},{19,3},{4,20},{20... | collective-permute-start | bytes 786440 | tf_op jit(solution)/shard_map/ppermute | solution.py:295
  156.5 14.4 %collective-permute-start.6 = (bf16[256,512]{1,0:T(8,128)(2,1)}, bf16[256,512]{1,0:T(8,128)(2,1)}, u32[]{:S(2)}, u32[]{:S(2)}) collective-permute-start(bf16[256,512]{1,0:T(8,128)(2,1)} %get-tuple-element.28), channel_id=1, source_target_pairs={{0,16},{16,0},{1,17},{17,1},{2,18},{18,2},{3,19},{19,3},{4,20},{20... | collective-permute-start | bytes 786440 | tf_op jit(solution)/shard_map/ppermute | solution.py:295
  164.0 7.3 %collective-permute-start.5 = (bf16[256,512]{1,0:T(8,128)(2,1)}, bf16[256,512]{1,0:T(8,128)(2,1)}, u32[]{:S(2)}, u32[]{:S(2)}) collective-permute-start(bf16[256,512]{1,0:T(8,128)(2,1)} %get-tuple-element.27), channel_id=1, source_target_pairs={{0,16},{16,0},{1,17},{17,1},{2,18},{18,2},{3,19},{19,3},{4,20},{20... | collective-permute-start | bytes 786440 | tf_op jit(solution)/shard_map/ppermute | solution.py:295
  170.7 7.0 %collective-permute-start.4 = (bf16[256,512]{1,0:T(8,128)(2,1)}, bf16[256,512]{1,0:T(8,128)(2,1)S(1)}, u32[]{:S(2)}, u32[]{:S(2)}) collective-permute-start(bf16[256,512]{1,0:T(8,128)(2,1)} %get-tuple-element.26), channel_id=1, source_target_pairs={{0,16},{16,0},{1,17},{17,1},{2,18},{18,2},{3,19},{19,3},{4,20},{20... | collective-permute-start | bytes 786440 | tf_op jit(solution)/shard_map/ppermute | solution.py:295
  179.7 3.0 collective-permute-start.8
  183.1 3.7 %copy-start.16 = (bf16[1024,512]{1,0:T(8,128)(2,1)}, bf16[1024,512]{1,0:T(8,128)(2,1)S(1)}, u32[]{:S(2)}) copy-start(bf16[1024,512]{1,0:T(8,128)(2,1)S(1)} %add_convert_fusion) | copy-start | bytes 3145732
  262.8 2.2 copy-start
  265.0 2.2 copy-start.4
  (5 other events, 4.7 us)
Sparse Core Ops, SparseCore 0:
  10.9 50.6 all-gather.4
  63.8 73.2 all-gather.6
  139.2 49.3 all-gather.8

commit v3 on v2

--- a/solution.py
+++ b/solution.py
@@ -15,6 +15,90 @@
 CHUNKS = 4
 MIB = 1 << 20
 MESH = pl.DeviceIdType.MESH
+
+
+def collect_kernel(
+    n, minors, in_ref, out_ref, local_sem, send1, recv1, send2, recv2, send3, recv3
+):
+    majors, length = n // (2 * minors), in_ref.shape[1]
+    me, side = lax.axis_index("col"), lax.axis_index("row")
+    core, chip = me % 2, me // 2
+    minor, major = chip % minors, chip // minors
+
+    def device(k, m, c):
+        return (((major + k) % majors) * minors + (minor + m) % minors) * 2 + c
+
+    def slot(at):
+        return out_ref.at[:, pl.ds(pl.multiple_of(at * length, length), length)]
+
+    def copy(source, at, sends, recvs, target):
+        return pltpu.make_async_remote_copy(
+            src_ref=source,
+            dst_ref=slot(at),
+            send_sem=sends,
+            recv_sem=recvs,
+            device_id=(side, target),
+            device_id_type=MESH,
+        )
+
+    peers = [device(k, 0, core) for k in range(1, majors)]
+    peers += [device(0, m, core) for m in range(1, minors)]
+    peers += [device(0, 0, 1 - core)]
+    barrier = pltpu.get_barrier_semaphore()
+    for peer in peers:
+        pl.semaphore_signal(barrier, inc=1, device_id=(side, peer), device_id_type=MESH)
+    pl.semaphore_wait(barrier, len(peers))
+
+    first = [
+        copy(in_ref, me, send1.at[k], recv1.at[k], device(k, 0, core)) for k in range(1, majors)
+    ]
+    for each in first:
+        each.start()
+    own = pltpu.make_async_copy(in_ref, slot(me), local_sem)
+    own.start()
+    second, third = {}, []
+    for k in range(majors):
+        at = device(majors - k, 0, core)
+        if k:
+            first[k - 1].wait_recv()
+        source = slot(at) if k else in_ref
+        for m in range(1, minors):
+            each = copy(source, at, send2.at[k, m], recv2.at[k, m], device(0, m, core))
+            each.start()
+            second[k, m] = each
+        each = copy(source, at, send3.at[k, 0], recv3.at[k, 0], device(0, 0, 1 - core))
+        each.start()
+        third.append(each)
+    for k in range(majors):
+        for m in range(1, minors):
+            at = device(majors - k, minors - m, core)
+            second[k, m].wait_recv()
+            each = copy(slot(at), at, send3.at[k, m], recv3.at[k, m], device(0, 0, 1 - core))
+            each.start()
+            third.append(each)
+    own.wait()
+    for each in first:
+        each.wait_send()
+    for each in second.values():
+        each.wait_send()
+    for each in third:
+        each.wait()
+
+
+def collect(value):
+    n = lax.axis_size("col")
+    minors = n // 8
+    kinds, length, width = value.shape
+    dma = pltpu.SemaphoreType.DMA
+    return pl.pallas_call(
+        functools.partial(collect_kernel, n, minors),
+        in_specs=[pl.BlockSpec(memory_space=pl.ANY)],
+        out_specs=pl.BlockSpec(memory_space=pl.ANY),
+        out_shape=jax.ShapeDtypeStruct((kinds, n * length, width), value.dtype),
+        scratch_shapes=[dma(())] + [dma((4,))] * 2 + [dma((4, minors))] * 4,
+        compiler_params=pltpu.CompilerParams(collective_id=2, has_side_effects=True),
+        name="collect",
+    )(value)
 
 
 def project_kernel(x_ref, w_ref, bias_ref, scale_ref, out_ref):
@@ -329,8 +413,8 @@
     def gather(value, axis):
         return lax.all_gather(value, "col", axis=axis, tiled=True)
 
-    w_first = gather(
-        jnp.concatenate([qkv_weight[0].transpose(1, 0, 2), out_weight.transpose(0, 2, 1)]), 1
+    w_first = collect(
+        jnp.concatenate([qkv_weight[0].transpose(1, 0, 2), out_weight.transpose(0, 2, 1)])
     )
     w_ffn = gather(jnp.concatenate([ffn_in, ffn_out.transpose(0, 2, 1)]), 1)
     w_cross = gather(cross_weight.transpose(0, 2, 1, 3), 2)

time: 300 us -> 296 us (0.987)
  waiting for transfers between devices: 89.5 us -> 16 us
  Pallas kernels: 148 us -> 215 us
  local copies, waits for them, and re-layouts: 20.1 us -> 17.1 us
    all_gather x3 -> x2, waiting for transfers between devices: 80 us -> 0.04 us  [gather(): return lax.all_gather(value, 'col', axis=axis, tiled=True)]
    pallas_call x0 -> x1, Pallas kernels: none -> 64.7 us  [collect(): pl.pallas_call(functools.partial(collect_kernel, n, minors), in_specs=[pl...]
    ppermute x9, waiting for transfers between devices: 9.4 us -> 16 us  [send(): lax.ppermute(value, 'row', [(i, (i + step) % count) for i in range(count)])]
    unnamed x54 -> x40, local copies, waits for them, and re-layouts: 19.3 us -> 16.3 us
  transfers between devices with their start and end apart: 12 -> 11, of which waited for: 5 -> 4; matrix products, arithmetic and copies ran while one was open for 5% -> 7% of each run, Pallas kernels for 41% -> 64%
where the time goes in v3:
time: 296 us; the launch traced here: 295 us
  Pallas kernels  215 us (73%)
  local copies, waits for them, and re-layouts  17.1 us (6%)
  waiting for transfers between devices  16 us (5%)
  between operations  15.1 us (5%)
  other arithmetic  10.9 us (4%)
  matrix products  7.61 us (3%)
  starting transfers between devices  7.45 us (3%)
  blocking collectives  6.49 us (2%)
    pallas_call x1, Pallas kernels, dispatch(): pl.pallas_call(functools.partial(dispatch_kernel, n, sides), in_specs=[pl...  76.3 us
    pallas_call x1, Pallas kernels, collect(): pl.pallas_call(functools.partial(collect_kernel, n, minors), in_specs=[pl...  64.7 us
    pallas_call x1, Pallas kernels, fill_cache(): pl.pallas_call(functools.partial(cache_kernel, pages=pages), grid_spec=pl...  26.1 us
    pallas_call x4, Pallas kernels, feed(): pl.pallas_call(feed_kernel, grid_spec=pltpu.PrefetchScalarGridSpec(num_sc...  23.9 us
    pallas_call x4, Pallas kernels, attention(): pl.pallas_call(attend_kernel, grid=(width // step,), in_specs=[pl.BlockSp...  19.8 us
    unnamed x40, local copies, waits for them, and re-layouts  16.3 us
    ppermute x9, waiting for transfers between devices, send(): lax.ppermute(value, 'row', [(i, (i + step) % count) for i in range(count)])  16 us
    ppermute x9, starting transfers between devices, send(): lax.ppermute(value, 'row', [(i, (i + step) % count) for i in range(count)])  7.37 us
  transfers between devices with their start and end apart: 11, of which 4 were waited for; matrix products, arithmetic and copies ran while one was open for 7% of the time, Pallas kernels for 64%

profile of v3, /device:TPU:25, one launch (start us, length us, event | category | flops | bytes accessed | tf_op | source)
XLA Modules:
  0.0 295.3 jit_solution(5860992112949867272)
XLA Ops:
  7.2 1.9 pad_maximum_fusion
  11.8 6.5 %all-reduce = s32[1024]{0:T(1024)S(1)} all-reduce(s32[1024]{0:T(1024)S(1)} %bitcast_dynamic-update-slice_fusion), channel_id=2, replica_groups=mesh['row'=2,'col'=16] {'col'}, use_global_device_ids=true, to_apply=%add | all-reduce | flops 1024 | bytes 8192
  18.8 1.3 fusion.12
  23.5 1.7 pad_maximum_fusion.1.in_ref
  25.2 64.7 %collect.1.w_ref = bf16[4,1024,512]{2,1,0:T(8,128)(2,1)} custom-call(bf16[4,64,512]{2,1,0:T(8,128)(2,1)} %pad_maximum_fusion.1.in_ref), custom_call_target="tpu_custom_call" | custom-call | tf_op jit(solution)/shard_map/collect/pallas_call | solution.py:93
  90.5 2.3 copy-done.1
  92.7 3.8 %project.1.q_ref.k_ref.v_ref = bf16[3,1024,512]{2,1,0:T(8,128)(2,1)S(1)} custom-call(bf16[1024,1024]{1,0:T(8,128)(2,1)S(1)} %copy-done.7, bf16[4,1024,512]{2,1,0:T(8,128)(2,1)S(1)} %copy-done.1, f32[3,1,512]{2,1,0:T(1,128)S(1)} %broadcast_in_dim.32.bias_ref, f32[3,1,512]{2,1,0:T(1,128)S(1)} %broadcast_in_dim.54.scale_ref), custom_call_target="tpu_custom_call" | custom-call | flops 5000000000 | bytes 8388608 | tf_op jit(solution)/shard_map/project/pallas_call | solution.py:112
  96.5 5.0 %attention.7 = bf16[256,512]{1,0:T(8,128)(2,1)S(1)} custom-call(bf16[3,1024,512]{2,1,0:T(8,128)(2,1)S(1)} %project.1.q_ref.k_ref.v_ref, bf16[3,1024,512]{2,1,0:T(8,128)(2,1)S(1)} %project.1.q_ref.k_ref.v_ref, bf16[3,1024,512]{2,1,0:T(8,128)(2,1)S(1)} %project.1.q_ref.k_ref.v_ref, s32[1024,1]{1,0:T(8,128)S(1)} %copy.25.seg_col_ref, s32[1,1024]{1,0:T(1,128)S(1)} %bitcast.59), custom_call_target="tpu_custom_call" | custom-call | flops 5000000000 | bytes 3145728 | tf_op jit(solution)/shard_map/attention/pallas_call | solution.py:156
  101.5 1.7 convolution_convert_fusion.mine_ref
  103.3 1.3 collective-permute-start.3
  105.3 1.9 copy-done.11
  107.2 5.0 %attention.6 = bf16[256,512]{1,0:T(8,128)(2,1)S(1)} custom-call(bf16[3,1024,512]{2,1,0:T(8,128)(2,1)S(1)} %copy-done.11, bf16[3,1024,512]{2,1,0:T(8,128)(2,1)S(1)} %copy-done.11, bf16[3,1024,512]{2,1,0:T(8,128)(2,1)S(1)} %copy-done.11, s32[1024,1]{1,0:T(8,128)S(1)} %copy.25.seg_col_ref, s32[1,1024]{1,0:T(1,128)S(1)} %bitcast.60), custom_call_target="tpu_custom_call" | custom-call | flops 5000000000 | bytes 3145728 | tf_op jit(solution)/shard_map/attention/pallas_call | solution.py:156
  112.2 1.3 convolution_convert_fusion.1.mine_ref
  113.7 5.0 %attention.5 = bf16[256,512]{1,0:T(8,128)(2,1)S(1)} custom-call(bf16[3,1024,512]{2,1,0:T(8,128)(2,1)S(1)} %copy-done.11, bf16[3,1024,512]{2,1,0:T(8,128)(2,1)S(1)} %copy-done.11, bf16[3,1024,512]{2,1,0:T(8,128)(2,1)S(1)} %copy-done.11, s32[1024,1]{1,0:T(8,128)S(1)} %copy.25.seg_col_ref, s32[1,1024]{1,0:T(1,128)S(1)} %bitcast.61), custom_call_target="tpu_custom_call" | custom-call | flops 5000000000 | bytes 3145728 | tf_op jit(solution)/shard_map/attention/pallas_call | solution.py:156
  120.4 5.0 %attention.4 = bf16[256,512]{1,0:T(8,128)(2,1)S(1)} custom-call(bf16[3,1024,512]{2,1,0:T(8,128)(2,1)S(1)} %copy-done.11, bf16[3,1024,512]{2,1,0:T(8,128)(2,1)S(1)} %copy-done.11, bf16[3,1024,512]{2,1,0:T(8,128)(2,1)S(1)} %copy-done.11, s32[1024,1]{1,0:T(8,128)S(1)} %copy.25.seg_col_ref, s32[1,1024]{1,0:T(1,128)S(1)} %bitcast.62), custom_call_target="tpu_custom_call" | custom-call | flops 5000000000 | bytes 3145728 | tf_op jit(solution)/shard_map/attention/pallas_call | solution.py:156
  126.4 3.4 %copy-done.4 = bf16[2,1024,2048]{2,1,0:T(8,128)(2,1)S(1)} copy-done((bf16[2,1024,2048]{2,1,0:T(8,128)(2,1)S(1)}, bf16[2,1024,2048]{2,1,0:T(8,128)(2,1)}, u32[]{:S(2)}) %copy-start.4) | copy-done | bytes 8388632
  129.8 1.6 copy-done.8
  131.4 5.8 %feed.7 = (bf16[256,512]{1,0:T(8,128)(2,1)S(1)}, bf16[256,512]{1,0:T(8,128)(2,1)S(1)}, bf16[256,512]{1,0:T(8,128)(2,1)S(1)}) custom-call(s32[1]{0:T(128)} %bitcast.side_ref, bf16[256,1024]{1,0:T(8,128)(2,1)S(1)} %convolution_convert_fusion.mine_ref, bf16[256,1024]{1,0:T(8,128)(2,1)} %collective-permute-done.3.theirs_ref, bf16[1024,1024]{1,0:T(8,128)(2,1)S(1)} %copy-done.8, ...), custom_call_target="tpu_custom_call" | custom-call | flops 8000000000 | bytes 10485760 | tf_op jit(solution)/shard_map/feed/pallas_call | solution.py:233
  138.4 6.4 %feed.6 = (bf16[256,512]{1,0:T(8,128)(2,1)S(1)}, bf16[256,512]{1,0:T(8,128)(2,1)}, bf16[256,512]{1,0:T(8,128)(2,1)S(1)}) custom-call(s32[1]{0:T(128)} %bitcast.side_ref, bf16[256,1024]{1,0:T(8,128)(2,1)} %convolution_convert_fusion.1.mine_ref, bf16[256,1024]{1,0:T(8,128)(2,1)} %collective-permute-done.2.theirs_ref, bf16[1024,1024]{1,0:T(8,128)(2,1)S(1)} %copy-done.8, ...), custom_call_target="tpu_custom_call" | custom-call | flops 8000000000 | bytes 10485760 | tf_op jit(solution)/shard_map/feed/pallas_call | solution.py:233
  145.1 6.3 %feed.5 = (bf16[256,512]{1,0:T(8,128)(2,1)S(1)}, bf16[256,512]{1,0:T(8,128)(2,1)}, bf16[256,512]{1,0:T(8,128)(2,1)S(1)}) custom-call(s32[1]{0:T(128)} %bitcast.side_ref, bf16[256,1024]{1,0:T(8,128)(2,1)S(1)} %convolution_convert_fusion.2.mine_ref, bf16[256,1024]{1,0:T(8,128)(2,1)} %collective-permute-done.1.theirs_ref, bf16[1024,1024]{1,0:T(8,128)(2,1)S(1)} %copy-done.8, ...), custom_call_target="tpu_custom_call" | custom-call | flops 8000000000 | bytes 10485760 | tf_op jit(solution)/shard_map/feed/pallas_call | solution.py:233
  152.6 5.4 %feed.4 = (bf16[256,512]{1,0:T(8,128)(2,1)S(1)}, bf16[256,512]{1,0:T(8,128)(2,1)}, bf16[256,512]{1,0:T(8,128)(2,1)S(1)}) custom-call(s32[1]{0:T(128)} %bitcast.side_ref, bf16[256,1024]{1,0:T(8,128)(2,1)S(1)} %convolution_convert_fusion.3.mine_ref, bf16[256,1024]{1,0:T(8,128)(2,1)S(1)} %collective-permute-done.theirs_ref, bf16[1024,1024]{1,0:T(8,128)(2,1)S(1)} %copy-done.8, ...), custom_call_target="tpu_custom_call" | custom-call | flops 8000000000 | bytes 10485760 | tf_op jit(solution)/shard_map/feed/pallas_call | solution.py:233
  158.3 3.5 %collective-permute-done.6 = bf16[256,512]{1,0:T(8,128)(2,1)} collective-permute-done((bf16[256,512]{1,0:T(8,128)(2,1)}, bf16[256,512]{1,0:T(8,128)(2,1)}, u32[]{:S(2)}, u32[]{:S(2)}) %collective-permute-start.6) | collective-permute-done | bytes 262176 | tf_op jit(solution)/shard_map/ppermute | solution.py:379
  161.8 5.6 %collective-permute-done.5 = bf16[256,512]{1,0:T(8,128)(2,1)} collective-permute-done((bf16[256,512]{1,0:T(8,128)(2,1)}, bf16[256,512]{1,0:T(8,128)(2,1)}, u32[]{:S(2)}, u32[]{:S(2)}) %collective-permute-start.5) | collective-permute-done | bytes 262176 | tf_op jit(solution)/shard_map/ppermute | solution.py:379
  167.4 5.5 %collective-permute-done.4 = bf16[256,512]{1,0:T(8,128)(2,1)S(1)} collective-permute-done((bf16[256,512]{1,0:T(8,128)(2,1)}, bf16[256,512]{1,0:T(8,128)(2,1)S(1)}, u32[]{:S(2)}, u32[]{:S(2)}) %collective-permute-start.4) | collective-permute-done | bytes 262176 | tf_op jit(solution)/shard_map/ppermute | solution.py:379
  172.9 2.0 fusion.15
  174.9 1.3 collective-permute-start.8
  176.2 1.3 collective-permute-done.8
  177.9 3.7 %fusion.2 = bf16[2048,512]{1,0:T(8,128)(2,1)} fusion(bf16[1024,512]{1,0:T(8,128)(2,1)S(1)} %add_convert_fusion, s32[1024]{0:T(1024)S(1)} %add.101), kind=kOutput, calls=%fused_computation.3 | convolution fusion | flops 2150629376 | bytes 3149824 | tf_op jit(solution)/shard_map/dot_general | solution.py:493
  181.6 76.3 %dispatch.1 = bf16[2,16,128,512]{3,2,1,0:T(8,128)(2,1)} custom-call(bf16[16,128,512]{2,1,0:T(8,128)(2,1)} %bitcast.63), custom_call_target="tpu_custom_call" | custom-call | tf_op jit(solution)/shard_map/dispatch/pallas_call | solution.py:321
  258.0 2.2 copy-done
  260.1 2.2 copy-done.6
  262.3 26.1 %fill_cache.1 = bf16[2,2304,2,512]{3,2,1,0:T(2,128)(2,1)} custom-call(s32[144]{0:T(256)S(1)} %select_reduce_fusion.index_ref, bf16[2,2048,512]{2,1,0:T(8,128)(2,1)S(1)} %bitcast.57, bf16[2,2,1024,512]{3,2,1,0:T(8,128)(2,1)S(1)} %copy-done.6), custom_call_target="tpu_custom_call" | custom-call | flops 10000000000 | bytes 18874368 | tf_op jit(solution)/shard_map/fill_cache/pallas_call | solution.py:356
  (86 shorter events, 13.6 us)
Async XLA Ops:
  7.2 119.2 %all-gather.4.cloned.1.call-start = ((), (), s32[]{:S(2)}) async-start(), calls=%async_computation | async-start | bytes 8912896 | tf_op jit(solution)/shard_map/all_gather | solution.py:414
  9.1 248.8 %all-gather.6.cloned.1.call-start = ((), (), s32[]{:S(2)}) async-start(), calls=%async_computation.1 | async-start | bytes 4456448 | tf_op jit(solution)/shard_map/all_gather | solution.py:414
  25.2 64.8 %copy-start.16 = (f32[1,2,512]{2,1,0:T(2,128)S(1)}, f32[1,2,512]{2,1,0:T(2,128)}, u32[]{:S(2)}) copy-start(f32[1,2,512]{2,1,0:T(2,128)} %param.17) | copy-start | bytes 12292
  25.2 64.9 %copy-start.3 = (s32[1024]{0:T(1024)S(1)}, s32[1024]{0:T(1024)}, u32[]{:S(2)}) copy-start(s32[1024]{0:T(1024)} %param.15) | copy-start | bytes 12292
  25.2 65.2 %copy-start.17 = (f32[3]{0:T(128)S(1)}, f32[3]{0:T(128)}, u32[]{:S(2)}) copy-start(f32[3]{0:T(128)} %constant.43.clone) | copy-start | bytes 40
  25.2 65.2 %copy-start.7 = (bf16[1024,1024]{1,0:T(8,128)(2,1)S(1)}, bf16[1024,1024]{1,0:T(8,128)(2,1)}, u32[]{:S(2)}) copy-start(bf16[1024,1024]{1,0:T(8,128)(2,1)} %x_ref.4) | copy-start | bytes 6291460
  90.5 2.3 copy-start.1
  96.5 5.0 %copy-start.10 = (bf16[3,1024,512]{2,1,0:T(8,128)(2,1)}, bf16[3,1024,512]{2,1,0:T(8,128)(2,1)S(1)}, u32[]{:S(2)}) copy-start(bf16[3,1024,512]{2,1,0:T(8,128)(2,1)S(1)} %project.1.q_ref.k_ref.v_ref) | copy-start | bytes 9437188
  101.5 3.0 %copy-start.13 = (bf16[2,64,2,512]{3,2,1,0:T(2,128)(2,1)S(1)}, bf16[2,64,2,512]{3,2,1,0:T(2,128)(2,1)}, u32[]{:S(2)}) copy-start(bf16[2,64,2,512]{3,2,1,0:T(2,128)(2,1)} %param.24) | copy-start | bytes 786436
  103.3 23.0 %collective-permute-start.3 = (bf16[256,1024]{1,0:T(8,128)(2,1)S(1)}, bf16[256,1024]{1,0:T(8,128)(2,1)}, u32[]{:S(2)}, u32[]{:S(2)}) collective-permute-start(bf16[256,1024]{1,0:T(8,128)(2,1)S(1)} %convolution_convert_fusion.mine_ref), channel_id=1, source_target_pairs={{0,16},{16,0},{1,17},{17,1},{2,18},{18,2},{3,19},{19,3},{4,20},{20... | collective-permute-start | bytes 1572872 | tf_op jit(solution)/shard_map/ppermute | solution.py:379
  105.3 1.9 copy-start.11
  107.2 5.0 %copy-start.2 = (bf16[4,1024,512]{2,1,0:T(8,128)(2,1)S(1)}, bf16[4,1024,512]{2,1,0:T(8,128)(2,1)}, u32[]{:S(2)}) copy-start(bf16[4,1024,512]{2,1,0:T(8,128)(2,1)} %collect.1.w_ref) | copy-start | bytes 12582916
  113.4 24.9 %collective-permute-start.2 = (bf16[256,1024]{1,0:T(8,128)(2,1)}, bf16[256,1024]{1,0:T(8,128)(2,1)}, u32[]{:S(2)}, u32[]{:S(2)}) collective-permute-start(bf16[256,1024]{1,0:T(8,128)(2,1)} %convolution_convert_fusion.1.mine_ref), channel_id=1, source_target_pairs={{0,16},{16,0},{1,17},{17,1},{2,18},{18,2},{3,19},{19,3},{4,20},{20... | collective-permute-start | bytes 1572872 | tf_op jit(solution)/shard_map/ppermute | solution.py:379
  119.2 7.1 %copy-start.15 = (f32[1,2,1024]{2,1,0:T(2,128)S(1)}, f32[1,2,1024]{2,1,0:T(2,128)}, u32[]{:S(2)}) copy-start(f32[1,2,1024]{2,1,0:T(2,128)} %param.22) | copy-start | bytes 24580
  119.2 7.1 %copy-start.14 = (f32[1,4,1024]{2,1,0:T(4,128)S(1)}, f32[1,4,1024]{2,1,0:T(4,128)}, u32[]{:S(2)}) copy-start(f32[1,4,1024]{2,1,0:T(4,128)} %param.23) | copy-start | bytes 49156
  119.2 25.9 %collective-permute-start.1 = (bf16[256,1024]{1,0:T(8,128)(2,1)S(1)}, bf16[256,1024]{1,0:T(8,128)(2,1)}, u32[]{:S(2)}, u32[]{:S(2)}) collective-permute-start(bf16[256,1024]{1,0:T(8,128)(2,1)S(1)} %convolution_convert_fusion.2.mine_ref), channel_id=1, source_target_pairs={{0,16},{16,0},{1,17},{17,1},{2,18},{18,2},{3,19},{19,3},{4,20},{20... | collective-permute-start | bytes 1572872 | tf_op jit(solution)/shard_map/ppermute | solution.py:379
  125.4 1.0 copy-start.9
  125.9 26.7 %collective-permute-start = (bf16[256,1024]{1,0:T(8,128)(2,1)S(1)}, bf16[256,1024]{1,0:T(8,128)(2,1)S(1)}, u32[]{:S(2)}, u32[]{:S(2)}) collective-permute-start(bf16[256,1024]{1,0:T(8,128)(2,1)S(1)} %convolution_convert_fusion.3.mine_ref), channel_id=1, source_target_pairs={{0,16},{16,0},{1,17},{17,1},{2,18},{18,2},{3,19},{19,3},{4,20},{20... | collective-permute-start | bytes 1572872 | tf_op jit(solution)/shard_map/ppermute | solution.py:379
  126.4 3.4 %copy-start.4 = (bf16[2,1024,2048]{2,1,0:T(8,128)(2,1)S(1)}, bf16[2,1024,2048]{2,1,0:T(8,128)(2,1)}, u32[]{:S(2)}) copy-start(bf16[2,1024,2048]{2,1,0:T(8,128)(2,1)} %all-gather.4.cloned.1.call-done.w_ref) | copy-start | bytes 25165828
  129.8 1.6 copy-start.8
  131.4 7.0 %copy-start.5 = (bf16[2,1024,2048]{2,1,0:T(8,128)(2,1)S(1)}, bf16[2,1024,2048]{2,1,0:T(8,128)(2,1)}, u32[]{:S(2)}) copy-start(bf16[2,1024,2048]{2,1,0:T(8,128)(2,1)} %all-gather.4.cloned.1.call-done.w_ref) | copy-start | bytes 25165828
  137.1 21.1 %collective-permute-start.7 = (bf16[256,512]{1,0:T(8,128)(2,1)S(1)}, bf16[256,512]{1,0:T(8,128)(2,1)}, u32[]{:S(2)}, u32[]{:S(2)}) collective-permute-start(bf16[256,512]{1,0:T(8,128)(2,1)S(1)} %get-tuple-element.29), channel_id=1, source_target_pairs={{0,16},{16,0},{1,17},{17,1},{2,18},{18,2},{3,19},{19,3},{4,20},{20... | collective-permute-start | bytes 786440 | tf_op jit(solution)/shard_map/ppermute | solution.py:379
  144.8 17.0 %collective-permute-start.6 = (bf16[256,512]{1,0:T(8,128)(2,1)}, bf16[256,512]{1,0:T(8,128)(2,1)}, u32[]{:S(2)}, u32[]{:S(2)}) collective-permute-start(bf16[256,512]{1,0:T(8,128)(2,1)} %get-tuple-element.28), channel_id=1, source_target_pairs={{0,16},{16,0},{1,17},{17,1},{2,18},{18,2},{3,19},{19,3},{4,20},{20... | collective-permute-start | bytes 786440 | tf_op jit(solution)/shard_map/ppermute | solution.py:379
  151.4 16.0 %collective-permute-start.5 = (bf16[256,512]{1,0:T(8,128)(2,1)}, bf16[256,512]{1,0:T(8,128)(2,1)}, u32[]{:S(2)}, u32[]{:S(2)}) collective-permute-start(bf16[256,512]{1,0:T(8,128)(2,1)} %get-tuple-element.27), channel_id=1, source_target_pairs={{0,16},{16,0},{1,17},{17,1},{2,18},{18,2},{3,19},{19,3},{4,20},{20... | collective-permute-start | bytes 786440 | tf_op jit(solution)/shard_map/ppermute | solution.py:379
  158.0 14.9 %collective-permute-start.4 = (bf16[256,512]{1,0:T(8,128)(2,1)}, bf16[256,512]{1,0:T(8,128)(2,1)S(1)}, u32[]{:S(2)}, u32[]{:S(2)}) collective-permute-start(bf16[256,512]{1,0:T(8,128)(2,1)} %get-tuple-element.26), channel_id=1, source_target_pairs={{0,16},{16,0},{1,17},{17,1},{2,18},{18,2},{3,19},{19,3},{4,20},{20... | collective-permute-start | bytes 786440 | tf_op jit(solution)/shard_map/ppermute | solution.py:379
  174.9 2.6 collective-permute-start.8
  177.9 3.7 %copy-start.12 = (bf16[1024,512]{1,0:T(8,128)(2,1)}, bf16[1024,512]{1,0:T(8,128)(2,1)S(1)}, u32[]{:S(2)}) copy-start(bf16[1024,512]{1,0:T(8,128)(2,1)S(1)} %add_convert_fusion) | copy-start | bytes 3145732
  257.9 2.2 copy-start
  260.1 2.2 copy-start.6
Sparse Core Ops, SparseCore 0:
  10.8 96.6 all-gather.3
  109.7 52.9 all-gather.5
